TPU v7x, 32 devices: a whole 2x2x4 slice. The times are simulated.
32 devices in a mesh: grp: 2 (over core), dom: 8 (over z, x), sub: 2 (over y).
Axes of the slice: x: 2, y: 2, z: 4, core: 2. Of those that a mesh axis runs over, the one named last changes fastest.
Arguments:
- positions: float32 [3, 8192], P(None, ('grp', 'dom', 'sub')), may hold values from 0 to 4
- charges: float32 [8192], P(('grp', 'dom', 'sub')), may hold values from -3 to 3
- polar: float32 [8192], P(('grp', 'dom', 'sub')), may hold values from 0.1 to 0.6
- features: bfloat16 [8192, 256], P(('grp', 'dom', 'sub')), may hold values from -6 to 6
- neighbours: int32 [8192, 32], P(('grp', 'dom', 'sub')), may hold values from 0 to 512, as said below
- send_rows: int32 [2, 4096], P(None, ('grp', 'dom', 'sub')), may hold values from 0 to 255
- blocks: int32 [128], P(('grp', 'dom', 'sub')), may hold values from 0 to 31
- radial_in: bfloat16 [2, 8, 64], replicated, may hold values from -2 to 2
- radial_mid: bfloat16 [2, 2, 64, 64], replicated, may hold values from -0.75 to 0.75
- radial_out: bfloat16 [2, 64, 256], replicated, may hold values from -0.75 to 0.75
- node_in: bfloat16 [2, 256, 256], replicated, may hold values from -0.375 to 0.375
- node_out: bfloat16 [2, 256, 256], replicated, may hold values from -0.375 to 0.375
- field_gain: float32 [256], replicated, may hold values from -3 to 3
- readout: bfloat16 [256, 2], replicated, may hold values from -0.375 to 0.375
Outputs:
- site_result: float32 [3, 8192], P(None, ('grp', 'dom', 'sub'))
- response: float32 [3, 8192], P(None, ('grp', 'dom', 'sub'))
Inputs may be any that keep to these rules, and one draw needn't show every extreme that they name: `neighbours`: entries below 256 name the block's own sites, entries from 256 to 511 its lent sites, 512 an empty slot; empty slots follow the used ones. `blocks`: repeats may occur.
All inputs are finite; a program needn't handle non-finite values.
Results may differ from a plain program's by a relative error of at most 0.0022.
The roundings to bfloat16 on the way count: a program that leaves them out, or rounds other values in their place, can miss the bound.
Values may be sent and summed in bfloat16 or wider, within the bound.
A program may use at most 64 MiB of HBM per device.

v0:
```python
import functools

import jax
import jax.numpy as jnp
from jax import lax
from jax.experimental import pallas as pl
from jax.experimental.pallas import tpu as pltpu
from jax.sharding import PartitionSpec as P

SWEEPS = 4
BLOCK = 128
SMOOTH = 1.0
SPACING = 0.75
MESH = pl.DeviceIdType.MESH
F32 = jnp.float32
BF16 = jnp.bfloat16


def silu(x):
    return x * (0.5 + 0.5 * jnp.tanh(0.5 * x))


def lane_pick(rows, index):
    shape = index.shape
    return jnp.take_along_axis(
        jnp.broadcast_to(rows, shape), index, axis=1, mode="promise_in_bounds"
    )


def table_gather(pieces, local, chunk):
    total = jnp.zeros(local.shape, F32)
    for number, rows in pieces:
        total = jnp.where(chunk == number, lane_pick(rows, local), total)
    return total


def kernel(
    n_dom,
    n_sub,
    positions,
    charges,
    polar,
    features,
    neighbours,
    send_rows,
    blocks,
    radial_in,
    radial_mid,
    radial_out,
    node_in,
    node_out,
    field_gain,
    readout,
    both,
    packet,
    everyone,
    near_rows,
    near_cols,
    own_rows,
    own_cols,
    extra_cols,
    rim_out,
    rim_in,
    geometry,
    hot,
    third,
    edge_weight,
    wide_in,
    wide_mid,
    wide_out,
    tables,
    lent,
    hidden_ref,
    acc,
    outside,
    pairs,
    terms,
    term_out,
    term_in,
    all_send,
    all_recv,
    rim_send,
    rim_recv,
    lift_send,
    lift_recv,
    term_send,
    term_recv,
):
    g = lax.axis_index("grp")
    p = lax.axis_index("dom") * n_sub + lax.axis_index("sub")
    site_result, response = both.at[0], both.at[1]
    n = n_dom * n_sub
    rows = positions.shape[1]
    own_blocks = rows // BLOCK
    slots = neighbours.shape[0]
    listed = blocks.shape[0]
    layers, basis, radial = radial_in.shape
    channels = features.shape[1]
    rim = send_rows.shape[1]
    pack = channels // radial
    groups = slots // pack
    other = 1 - g

    def place(group, q):
        return (group, lax.div(q, n_sub), lax.rem(q, n_sub))

    def peer(i):
        return lax.rem(p + i, n)

    barrier = pltpu.get_barrier_semaphore()

    @pl.loop(0, n)
    def _(i):
        pl.semaphore_signal(barrier, inc=1, device_id=place(other, peer(i)), device_id_type=MESH)

    @pl.when(p > 0)
    def _():
        pl.semaphore_signal(barrier, inc=1, device_id=place(g, p - 1), device_id_type=MESH)

    @pl.when(p < n - 1)
    def _():
        pl.semaphore_signal(barrier, inc=1, device_id=place(g, p + 1), device_id_type=MESH)

    own_rows[...] = jnp.zeros_like(own_rows)
    own_rows[0:3, :] = positions[...]
    own_rows[3:4, :] = charges[...]
    own = own_rows[...]
    for b in range(own_blocks):
        packet[b] = own[:, b * BLOCK : (b + 1) * BLOCK]

    def fill_rims(step, values):
        for side in range(2):
            index = jnp.broadcast_to(send_rows[side : side + 1, :], (8, rim))
            rim_out[step, side] = table_gather(
                [(c, values[:, c * BLOCK : (c + 1) * BLOCK]) for c in range(own_blocks)],
                index & (BLOCK - 1),
                lax.shift_right_logical(index, 7),
            )

    def side_copy(src, dst, send, recv, step, side, q):
        return pltpu.make_async_remote_copy(
            src_ref=src,
            dst_ref=dst,
            send_sem=send.at[step, side],
            recv_sem=recv.at[step, side],
            device_id=place(g, q),
            device_id_type=MESH,
        )

    def rim_copy(step, side, q):
        return side_copy(
            rim_out.at[step, side], rim_in.at[step, side], rim_send, rim_recv, step, side, q
        )

    def lift_copy(layer, side, q):
        return side_copy(
            lent.at[layer, side],
            tables.at[layer, pl.ds(rows + side * rim, rim)],
            lift_send,
            lift_recv,
            layer,
            side,
            q,
        )

    def start(copy, step):
        @pl.when(p < n - 1)
        def _():
            copy(step, 0, p + 1).start()

        @pl.when(p > 0)
        def _():
            copy(step, 1, p - 1).start()

    def arrive(copy, step):
        @pl.when(p > 0)
        def _():
            copy(step, 0, p - 1).wait_recv()

        @pl.when(p < n - 1)
        def _():
            copy(step, 1, p + 1).wait_recv()

    def gone(copy, step):
        @pl.when(p < n - 1)
        def _():
            copy(step, 0, p + 1).wait_send()

        @pl.when(p > 0)
        def _():
            copy(step, 1, p - 1).wait_send()

    fill_rims(0, own)

    @pl.when(p == 0)
    def _():
        for step in range(1 + SWEEPS):
            rim_in[step, 0] = jnp.zeros((8, rim), F32)
        for layer in range(layers):
            tables[layer, rows : rows + rim] = jnp.zeros((rim, channels), BF16)

    @pl.when(p == n - 1)
    def _():
        for step in range(1 + SWEEPS):
            rim_in[step, 1] = jnp.zeros((8, rim), F32)
        for layer in range(layers):
            tables[layer, rows + rim :] = jnp.zeros((rim, channels), BF16)

    pl.semaphore_wait(barrier, n + (p > 0).astype(jnp.int32) + (p < n - 1).astype(jnp.int32))

    def packet_copy(i):
        return pltpu.make_async_remote_copy(
            src_ref=packet,
            dst_ref=everyone.at[pl.ds(p * own_blocks, own_blocks)],
            send_sem=all_send,
            recv_sem=all_recv,
            device_id=place(other, peer(i)),
            device_id_type=MESH,
        )

    start(rim_copy, 0)

    @pl.loop(0, n)
    def _(i):
        packet_copy(i).start()

    own_cols[...] = own.T

    def field(targets, source_cols, count, charge, dipole):
        x, y, z = (targets[c : c + 1, :] for c in range(3))
        width = targets.shape[1]

        def step(i, sums):
            at = pl.ds(pl.multiple_of(i * 8, 8), 8)
            source = source_cols[at, :]
            rx = x - source[:, 0:1]
            ry = y - source[:, 1:2]
            rz = z - source[:, 2:3]
            w = lax.rsqrt(rx * rx + ry * ry + rz * rz + SMOOTH)
            w2 = w * w
            w3 = w2 * w
            if not dipole:
                s = charge(at, source) * w3
                return (sums[0] + rx * s, sums[1] + ry * s, sums[2] + rz * s)
            d = extra_cols[at, :]
            dx, dy, dz = d[:, 0:1], d[:, 1:2], d[:, 2:3]
            s = 3.0 * (rx * dx + ry * dy + rz * dz) * (w3 * w2)
            return (
                sums[0] + (rx * s - dx * w3),
                sums[1] + (ry * s - dy * w3),
                sums[2] + (rz * s - dz * w3),
            )

        zero = jnp.zeros((8, width), F32)
        sums = lax.fori_loop(0, count // 8, step, (zero, zero, zero), unroll=16)
        return [jnp.sum(s, axis=0, keepdims=True) for s in sums]

    def edges():
        arrive(rim_copy, 0)
        for tile in range(own_blocks):
            at = slice(tile * BLOCK, (tile + 1) * BLOCK)
            index = neighbours[:, at]
            local = index & (BLOCK - 1)
            chunk = lax.shift_right_logical(index, 7)
            picked = []
            for c in range(4):
                pieces = [
                    (b, own_rows[c : c + 1, b * BLOCK : (b + 1) * BLOCK])
                    for b in range(own_blocks)
                ] + [(own_blocks + side, rim_in[0, side, c : c + 1, :]) for side in range(2)]
                picked.append(table_gather(pieces, local, chunk))
            ox, oy, oz = (own_rows[c : c + 1, at] - picked[c] for c in range(3))
            dist_sq = ox * ox + oy * oy + oz * oz + SMOOTH
            yield at, (ox, oy, oz), dist_sq, picked[3], local, chunk

    def send_terms(charge, dipole):
        width = listed * BLOCK
        for half in range(0, width, 2 * BLOCK):
            out = field(
                near_rows[:, half : half + 2 * BLOCK], own_cols, rows, charge, dipole
            )
            for c in range(3):
                terms[c : c + 1, half : half + 2 * BLOCK] = out[c]

    centre = lax.broadcasted_iota(jnp.int32, (basis, rows), 0).astype(F32) * SPACING

    def radial_step(q, layer):
        parts = []
        for j in range(pack):
            away = jnp.broadcast_to(geometry[0, pl.ds(q * pack + j, 1), :], (basis, rows))
            away = away - centre
            parts.append(jnp.exp(-(away * away)))
        wave = jnp.concatenate(parts, axis=0).astype(BF16)
        h = lax.dot_general(
            wave, wide_in[layer], (((0,), (0,)), ((), ())), preferred_element_type=F32
        )
        h = silu(h).astype(BF16)
        for m in range(2):
            h = silu(jnp.dot(h, wide_mid[layer, m], preferred_element_type=F32)).astype(BF16)
        third[layer, q] = h

    def radial_net(layer):
        @pl.loop(0, groups, unroll=4)
        def _(q):
            radial_step(q, layer)

    def edge_net(layer):
        @pl.loop(0, pack)
        def _(j):
            weight = jnp.dot(
                third[layer].reshape(groups * rows, channels),
                wide_out[layer, j],
                preferred_element_type=F32,
            )
            edge_weight[j] = weight.reshape(groups, rows, channels)

    @pl.when(g == 0)
    def _():
        lane = lax.broadcasted_iota(jnp.int32, (rows, rows + 2 * rim), 1)
        listing = jnp.concatenate(
            [neighbours[...].astype(F32), jnp.zeros((BLOCK - slots, rows), F32)], axis=0
        ).T.astype(jnp.int32)
        for k in range(slots):
            hot[k % pack, k // pack] = jnp.where(listing[:, k : k + 1] == lane, 1.0, 0.0).astype(BF16)
        spread_r = (
            lax.broadcasted_iota(jnp.int32, (channels, radial), 0) % radial
            == lax.broadcasted_iota(jnp.int32, (channels, radial), 1)
        ).astype(F32).astype(BF16)
        spread_c = (
            lax.broadcasted_iota(jnp.int32, (radial, channels), 1) % radial
            == lax.broadcasted_iota(jnp.int32, (radial, channels), 0)
        ).astype(F32).astype(BF16)
        same_in = (
            lax.broadcasted_iota(jnp.int32, (pack * basis, channels), 0) // basis
            == lax.broadcasted_iota(jnp.int32, (pack * basis, channels), 1) // radial
        )
        same_mid = (
            lax.broadcasted_iota(jnp.int32, (channels, channels), 0) // radial
            == lax.broadcasted_iota(jnp.int32, (channels, channels), 1) // radial
        )
        for layer in range(layers):
            flat = jnp.dot(radial_in[layer], spread_c, preferred_element_type=F32)
            wide_in[layer] = jnp.where(
                same_in, jnp.concatenate([flat] * pack, axis=0), 0.0
            ).astype(BF16)
            for m in range(2):
                flat = jnp.dot(
                    jnp.dot(spread_r, radial_mid[layer, m], preferred_element_type=F32).astype(
                        BF16
                    ),
                    spread_c,
                    preferred_element_type=F32,
                )
                wide_mid[layer, m] = jnp.where(same_mid, flat, 0.0).astype(BF16)
            for j in range(pack):
                wide_out[layer, j] = jnp.zeros((channels, channels), BF16)
                wide_out[layer, j, j * radial : (j + 1) * radial, :] = radial_out[layer]
        for at, _, dist_sq, _, _, _ in edges():
            geometry[0, :, at] = jnp.sqrt(dist_sq)
        radial_net(0)

    @pl.when(g == 1)
    def _():
        for at, offset, dist_sq, source_charge, _, _ in edges():
            w = lax.rsqrt(dist_sq)
            w2 = w * w
            w3 = w2 * w
            s = source_charge * w3
            for c in range(3):
                geometry[c, :, at] = offset[c]
                extra = jnp.sum(offset[c] * s, axis=0, keepdims=True)
                pairs[c : c + 1, at] = extra
            geometry[3, :, at] = w3
            geometry[4, :, at] = 3.0 * (w3 * w2)

    pltpu.make_async_copy(everyone, everyone, all_recv).wait()
    for l in range(listed):
        tile = everyone[blocks[l]]
        near_rows[:, l * BLOCK : (l + 1) * BLOCK] = tile
        near_cols[l * BLOCK : (l + 1) * BLOCK, :] = tile.T

    out = field(own, near_cols, listed * BLOCK, lambda at, source: source[:, 3:4], False)
    for c in range(3):
        outside[c : c + 1, :] = out[c]

    @pl.when(g == 0)
    def _():
        fx, fy, fz = out
        strength = jnp.sqrt(1.0 + fx * fx + fy * fy + fz * fz)
        site_result[2:3, :] = strength
        strength_col = jnp.broadcast_to(strength, (8, rows)).T[:, 0:1]
        hidden_ref[...] = (features[...].astype(F32) + strength_col * field_gain[...]).astype(BF16)

        def lift(layer):
            lifted = jnp.dot(
                hidden_ref[...], node_in[layer], preferred_element_type=F32
            ).astype(BF16)
            site = lax.broadcasted_iota(jnp.int32, (rows, rim), 0)
            for side in range(2):
                pick = jnp.where(site == send_rows[side : side + 1, :], 1.0, 0.0).astype(BF16)
                lent[layer, side] = lax.dot_general(
                    pick, lifted, (((0,), (0,)), ((), ())), preferred_element_type=F32
                ).astype(BF16)
            start(lift_copy, layer)
            tables[layer, 0:rows] = lifted

        for layer in range(layers):
            lift(layer)
            edge_net(layer)
            if layer + 1 < layers:
                radial_net(layer + 1)
            arrive(lift_copy, layer)
            acc[...] = jnp.zeros_like(acc)

            @pl.loop(0, pack, unroll=2)
            def _(j):
                source = jnp.dot(
                    hot[j].reshape(groups * rows, rows + 2 * rim),
                    tables[layer],
                    preferred_element_type=F32,
                )
                product = edge_weight[j] * source.reshape(groups, rows, channels)
                acc[...] += jnp.sum(product, axis=0)

            message = (acc[...] * (1.0 / slots)).astype(BF16)
            update = silu(jnp.dot(message, node_out[layer], preferred_element_type=F32))
            hidden_ref[...] = (hidden_ref[...].astype(F32) + update).astype(BF16)

        across = (((1,), (1,)), ((), ()))
        extra_cols[:, 0:2] = lax.dot_general(
            hidden_ref[...], readout[...], across, preferred_element_type=F32
        )
        site_result[0:2, :] = lax.dot_general(
            readout[...], hidden_ref[...], across, preferred_element_type=F32
        )
        send_terms(lambda at, source: extra_cols[at, 0:1], False)
        for layer in range(layers):
            gone(lift_copy, layer)

    @pl.when(g == 1)
    def _():
        gain = polar[...]
        outside[...] = outside[...] + pairs[...]
        dipole = [gain * outside[c : c + 1, :] for c in range(3)]
        for sweep in range(SWEEPS):
            step = 1 + sweep
            stacked = jnp.concatenate(dipole + [jnp.zeros((5, rows), F32)], axis=0)
            fill_rims(step, stacked)
            start(rim_copy, step)
            arrive(rim_copy, step)
            fresh = [[], [], []]
            for tile in range(own_blocks):
                at = slice(tile * BLOCK, (tile + 1) * BLOCK)
                index = neighbours[:, at]
                local = index & (BLOCK - 1)
                chunk = lax.shift_right_logical(index, 7)
                d = []
                for c in range(3):
                    pieces = [
                        (b, dipole[c][:, b * BLOCK : (b + 1) * BLOCK]) for b in range(own_blocks)
                    ] + [
                        (own_blocks + side, rim_in[step, side, c : c + 1, :]) for side in range(2)
                    ]
                    d.append(table_gather(pieces, local, chunk))
                r = [geometry[c, :, at] for c in range(3)]
                w3 = geometry[3, :, at]
                s = (r[0] * d[0] + r[1] * d[1] + r[2] * d[2]) * geometry[4, :, at]
                for c in range(3):
                    total = jnp.sum(r[c] * s - d[c] * w3, axis=0, keepdims=True)
                    fresh[c].append(gain[:, at] * (outside[c : c + 1, at] + total))
            dipole = [jnp.concatenate(f, axis=1) for f in fresh]
        for c in range(3):
            site_result[c : c + 1, :] = dipole[c]
        stacked = jnp.concatenate(dipole + [jnp.zeros((5, rows), F32)], axis=0)
        extra_cols[...] = stacked.T
        send_terms(None, True)
        for sweep in range(SWEEPS):
            gone(rim_copy, 1 + sweep)

    @pl.loop(0, n)
    def _(q):
        for b in range(own_blocks):
            total = jnp.zeros((3, BLOCK), F32)
            for l in range(listed):
                total = total + jnp.where(
                    blocks[l] == q * own_blocks + b, terms[:, l * BLOCK : (l + 1) * BLOCK], 0.0
                )
            term_out[q, b * 3 : (b + 1) * 3, :] = total

    def term_copy(i):
        return pltpu.make_async_remote_copy(
            src_ref=term_out.at[peer(i)],
            dst_ref=term_in.at[p],
            send_sem=term_send,
            recv_sem=term_recv,
            device_id=place(other, peer(i)),
            device_id_type=MESH,
        )

    @pl.loop(0, n)
    def _(i):
        term_copy(i).start()

    gone(rim_copy, 0)
    pltpu.make_async_copy(everyone, everyone, all_send).wait()
    pltpu.make_async_copy(term_in, term_in, term_recv).wait()

    total = jnp.sum(term_in[...], axis=0)
    for b in range(own_blocks):
        response[:, b * BLOCK : (b + 1) * BLOCK] = total[b * 3 : (b + 1) * 3, :]
    pltpu.make_async_copy(term_in, term_in, term_send).wait()


def local(n_dom, n_sub, *args):
    (
        positions,
        charges,
        polar,
        features,
        neighbours,
        send_rows,
        blocks,
        radial_in,
        radial_mid,
        radial_out,
        node_in,
        node_out,
        field_gain,
        readout,
    ) = args
    n = n_dom * n_sub
    rows = positions.shape[1]
    own_blocks = rows // BLOCK
    slots = neighbours.shape[1]
    listed = blocks.shape[0]
    layers, basis, radial = radial_in.shape
    channels = features.shape[1]
    rim = send_rows.shape[1]
    pack = channels // radial
    vmem = pl.BlockSpec(memory_space=pltpu.VMEM)
    specs = [vmem] * 14
    specs[6] = pl.BlockSpec(memory_space=pltpu.SMEM)
    dma = pltpu.SemaphoreType.DMA
    both = pl.pallas_call(
        functools.partial(kernel, n_dom, n_sub),
        out_shape=jax.ShapeDtypeStruct((2, 3, rows), F32),
        in_specs=specs,
        out_specs=vmem,
        scratch_shapes=[
            pltpu.VMEM((own_blocks, 8, BLOCK), F32),
            pltpu.VMEM((n * own_blocks, 8, BLOCK), F32),
            pltpu.VMEM((8, listed * BLOCK), F32),
            pltpu.VMEM((listed * BLOCK, 8), F32),
            pltpu.VMEM((8, rows), F32),
            pltpu.VMEM((rows, 8), F32),
            pltpu.VMEM((rows, 8), F32),
            pltpu.VMEM((1 + SWEEPS, 2, 8, rim), F32),
            pltpu.VMEM((1 + SWEEPS, 2, 8, rim), F32),
            pltpu.VMEM((5, slots, rows), F32),
            pltpu.VMEM((pack, slots // pack, rows, rows + 2 * rim), BF16),
            pltpu.VMEM((layers, slots // pack, rows, channels), BF16),
            pltpu.VMEM((pack, slots // pack, rows, channels), F32),
            pltpu.VMEM((layers, pack * basis, channels), BF16),
            pltpu.VMEM((layers, 2, channels, channels), BF16),
            pltpu.VMEM((layers, pack, channels, channels), BF16),
            pltpu.VMEM((layers, rows + 2 * rim, channels), BF16),
            pltpu.VMEM((layers, 2, rim, channels), BF16),
            pltpu.VMEM((rows, channels), BF16),
            pltpu.VMEM((rows, channels), F32),
            pltpu.VMEM((3, rows), F32),
            pltpu.VMEM((3, rows), F32),
            pltpu.VMEM((3, listed * BLOCK), F32),
            pltpu.VMEM((n, own_blocks * 3, BLOCK), F32),
            pltpu.VMEM((n, own_blocks * 3, BLOCK), F32),
            dma(()),
            dma(()),
            dma((1 + SWEEPS, 2)),
            dma((1 + SWEEPS, 2)),
            dma((layers, 2)),
            dma((layers, 2)),
            dma(()),
            dma(()),
        ],
        compiler_params=pltpu.CompilerParams(
            collective_id=0, has_side_effects=True, vmem_limit_bytes=56 * 2**20
        ),
    )(
        positions,
        charges.reshape(1, -1),
        polar.reshape(1, -1),
        features,
        neighbours.T,
        send_rows,
        blocks,
        radial_in,
        radial_mid,
        radial_out,
        node_in,
        node_out,
        field_gain.reshape(1, -1),
        readout.T,
    )
    return both[0], both[1]


def solution(mesh):
    sites = ("grp", "dom", "sub")
    in_specs = (
        P(None, sites),
        P(sites),
        P(sites),
        P(sites, None),
        P(sites, None),
        P(None, sites),
        P(sites),
    ) + (P(),) * 7
    out_specs = (P(None, sites), P(None, sites))
    body = functools.partial(local, mesh.shape["dom"], mesh.shape["sub"])
    return jax.shard_map(body, mesh=mesh, in_specs=in_specs, out_specs=out_specs, check_vma=False)
```

profile of v0, /device:TPU:1, one launch (start us, length us, event | category | flops | bytes accessed | tf_op | source)
XLA Modules:
  0.0 36.8 jit_solution(8033037425525942304)
XLA Ops:
  0.6 34.9 %shard_map.149 = f32[2,3,256]{2,1,0:T(4,128)} custom-call(f32[3,256]{1,0:T(4,128)} %positions.1, f32[1,256]{1,0:T(1,128)} %bitcast.10, f32[1,256]{1,0:T(1,128)} %bitcast.11, bf16[256,256]{1,0:T(8,128)(2,1)} %features.1, s32[32,256]{1,0:T(8,128)} %bitcast.9, s32[2,128]{1,0:T(2,128)} %send_rows.1, s32[4]{0:T(128)} %blocks.1, bf16[2,8,64]{2,1,0:T(8,128)(2,1)} %radial_in.1, ...), custom_call_target="tpu_custom_call" | custom-call | tf_op jit(solution)/shard_map/pallas_call | solution.py:544
  35.5 1.3 %slice_bitcast_fusion = (f32[3,256]{1,0:T(4,128)}, f32[3,256]{1,0:T(4,128)}) fusion(f32[2,3,256]{2,1,0:T(4,128)} %shard_map.149), kind=kLoop, calls=%fused_computation | loop fusion | bytes 12288 | tf_op jit(solution)/shard_map/squeeze | solution.py:603
where the time goes:
time: 37 us; the launch traced here: 36.8 us
  Pallas kernels  34.9 us (94%)
  local copies, waits for them, and re-layouts  1.28 us (3%)
  between operations  0.64 us (2%)
    pallas_call x1, Pallas kernels, local(): pl.pallas_call(functools.partial(kernel, n_dom, n_sub), out_shape=jax.Sha...  34.9 us
    squeeze x1, local copies, waits for them, and re-layouts, local(): return (both[0], both[1])  1.28 us

commit v1 on v0

--- a/solution.py
+++ b/solution.py
@@ -12,12 +12,14 @@
 SMOOTH = 1.0
 SPACING = 0.75
 MESH = pl.DeviceIdType.MESH
+INPUTS = 14
+STRIP = 16
 F32 = jnp.float32
 BF16 = jnp.bfloat16
 
 
-def silu(x):
-    return x * (0.5 + 0.5 * jnp.tanh(0.5 * x))
+def silu_of_half(half):
+    return half + half * jnp.tanh(half)
 
 
 def lane_pick(rows, index):
@@ -37,6 +39,11 @@
 def kernel(
     n_dom,
     n_sub,
+    *refs,
+):
+    sources = refs[:INPUTS]
+    (
+    both,
     positions,
     charges,
     polar,
@@ -51,7 +58,7 @@
     node_out,
     field_gain,
     readout,
-    both,
+    in_sem,
     packet,
     everyone,
     near_rows,
@@ -63,6 +70,9 @@
     rim_in,
     geometry,
     hot,
+    pick,
+    wave,
+    stage,
     third,
     edge_weight,
     wide_in,
@@ -85,7 +95,7 @@
     lift_recv,
     term_send,
     term_recv,
-):
+    ) = refs[INPUTS:]
     g = lax.axis_index("grp")
     p = lax.axis_index("dom") * n_sub + lax.axis_index("sub")
     site_result, response = both.at[0], both.at[1]
@@ -99,7 +109,32 @@
     rim = send_rows.shape[1]
     pack = channels // radial
     groups = slots // pack
+    strips = rows // STRIP
     other = 1 - g
+    held = (
+        positions,
+        charges,
+        polar,
+        features,
+        neighbours,
+        send_rows,
+        blocks,
+        radial_in,
+        radial_mid,
+        radial_out,
+        node_in,
+        node_out,
+        field_gain,
+        readout,
+    )
+    early = (0, 1, 2, 4, 5, 6)
+    late = (7, 8, 9, 3, 10, 11, 12, 13)
+
+    def load(number):
+        return pltpu.make_async_copy(sources[number], held[number], in_sem.at[number])
+
+    for number in early:
+        load(number).start()
 
     def place(group, q):
         return (group, lax.div(q, n_sub), lax.rem(q, n_sub))
@@ -121,7 +156,14 @@
     def _():
         pl.semaphore_signal(barrier, inc=1, device_id=place(g, p + 1), device_id_type=MESH)
 
+    @pl.when(g == 0)
+    def _():
+        for number in late:
+            load(number).start()
+
     own_rows[...] = jnp.zeros_like(own_rows)
+    for number in early:
+        load(number).wait()
     own_rows[0:3, :] = positions[...]
     own_rows[3:4, :] = charges[...]
     own = own_rows[...]
@@ -190,6 +232,62 @@
         def _():
             copy(step, 1, p - 1).wait_send()
 
+    def prepare():
+        width = rows + 2 * rim
+        lane = lax.broadcasted_iota(jnp.int32, (rows, width), 1).astype(jnp.int16)
+        listing = jnp.concatenate(
+            [neighbours[...].astype(F32), jnp.zeros((BLOCK - slots, rows), F32)], axis=0
+        ).T.astype(jnp.int32)
+        one, none = jnp.ones((rows, width), BF16), jnp.zeros((rows, width), BF16)
+        for k in range(slots):
+            entry = jnp.broadcast_to(listing[:, k : k + 1], (rows, BLOCK)).astype(jnp.int16)
+            entry = jnp.concatenate([entry] * (width // BLOCK), axis=1)
+            mark = jnp.where(entry == lane, one, none)
+            hot[k % pack, :, k // pack] = mark.reshape(strips, STRIP, width)
+        lists = jnp.concatenate(
+            [send_rows[...].astype(F32), jnp.zeros((6, rim), F32)], axis=0
+        ).T.astype(jnp.int32)
+        site = lax.broadcasted_iota(jnp.int32, (rim, rows), 1)
+        for side in range(2):
+            pick[side * rim : (side + 1) * rim, :] = jnp.where(
+                lists[:, side : side + 1] == site, 1.0, 0.0
+            ).astype(BF16)
+        for number in late[:3]:
+            load(number).wait()
+        spread_r = (
+            lax.broadcasted_iota(jnp.int32, (channels, radial), 0) % radial
+            == lax.broadcasted_iota(jnp.int32, (channels, radial), 1)
+        ).astype(F32).astype(BF16)
+        spread_c = (
+            lax.broadcasted_iota(jnp.int32, (radial, channels), 1) % radial
+            == lax.broadcasted_iota(jnp.int32, (radial, channels), 0)
+        ).astype(F32).astype(BF16)
+        same_in = (
+            lax.broadcasted_iota(jnp.int32, (pack * basis, channels), 0) // basis
+            == lax.broadcasted_iota(jnp.int32, (pack * basis, channels), 1) // radial
+        )
+        same_mid = (
+            lax.broadcasted_iota(jnp.int32, (channels, channels), 0) // radial
+            == lax.broadcasted_iota(jnp.int32, (channels, channels), 1) // radial
+        )
+        for layer in range(layers):
+            flat = jnp.dot(radial_in[layer], spread_c, preferred_element_type=F32)
+            wide_in[layer] = jnp.where(
+                same_in, jnp.concatenate([0.5 * flat] * pack, axis=0), 0.0
+            ).astype(BF16)
+            for m in range(2):
+                flat = jnp.dot(
+                    jnp.dot(spread_r, radial_mid[layer, m], preferred_element_type=F32).astype(
+                        BF16
+                    ),
+                    spread_c,
+                    preferred_element_type=F32,
+                )
+                wide_mid[layer, m] = jnp.where(same_mid, 0.5 * flat, 0.0).astype(BF16)
+            for j in range(pack):
+                wide_out[layer, j] = jnp.zeros((channels, channels), BF16)
+                wide_out[layer, j, j * radial : (j + 1) * radial, :] = radial_out[layer]
+
     fill_rims(0, own)
 
     @pl.when(p == 0)
@@ -205,6 +303,10 @@
             rim_in[step, 1] = jnp.zeros((8, rim), F32)
         for layer in range(layers):
             tables[layer, rows + rim :] = jnp.zeros((rim, channels), BF16)
+
+    @pl.when(g == 0)
+    def _():
+        prepare()
 
     pl.semaphore_wait(barrier, n + (p > 0).astype(jnp.int32) + (p < n - 1).astype(jnp.int32))
 
@@ -284,80 +386,64 @@
 
     centre = lax.broadcasted_iota(jnp.int32, (basis, rows), 0).astype(F32) * SPACING
 
-    def radial_step(q, layer):
-        parts = []
+    def radial_net():
+        half = groups // 2
+        spans = [range(half), range(half, groups)]
+        for q in range(groups):
+            parts = []
+            for j in range(pack):
+                away = jnp.broadcast_to(geometry[0, q * pack + j : q * pack + j + 1, :], (basis, rows))
+                away = away - centre
+                parts.append(jnp.exp(-(away * away)))
+            turned = jnp.concatenate(parts, axis=0).T
+            wave[q * rows : (q + 1) * rows, :] = turned.astype(BF16)
+        for layer in range(layers):
+            for step in range(3):
+                for part, span in enumerate(spans):
+                    at = slice(span[0] * rows, (span[-1] + 1) * rows)
+                    if step == 0:
+                        source, weight = wave[at, :], wide_in[layer]
+                    else:
+                        source, weight = stage[layer, step - 1, at, :], wide_mid[layer, step - 1]
+                    h = silu_of_half(jnp.dot(source, weight, preferred_element_type=F32)).astype(BF16)
+                    if step < 2:
+                        stage[layer, step, at, :] = h
+                    else:
+                        for i, q in enumerate(span):
+                            third[layer, :, q] = h[i * rows : (i + 1) * rows].reshape(
+                                strips, STRIP, channels
+                            )
+
+    def own_part(layer):
         for j in range(pack):
-            away = jnp.broadcast_to(geometry[0, pl.ds(q * pack + j, 1), :], (basis, rows))
-            away = away - centre
-            parts.append(jnp.exp(-(away * away)))
-        wave = jnp.concatenate(parts, axis=0).astype(BF16)
-        h = lax.dot_general(
-            wave, wide_in[layer], (((0,), (0,)), ((), ())), preferred_element_type=F32
-        )
-        h = silu(h).astype(BF16)
-        for m in range(2):
-            h = silu(jnp.dot(h, wide_mid[layer, m], preferred_element_type=F32)).astype(BF16)
-        third[layer, q] = h
-
-    def radial_net(layer):
-        @pl.loop(0, groups, unroll=4)
-        def _(q):
-            radial_step(q, layer)
-
-    def edge_net(layer):
-        @pl.loop(0, pack)
-        def _(j):
-            weight = jnp.dot(
+            edge_weight[j] = jnp.dot(
                 third[layer].reshape(groups * rows, channels),
                 wide_out[layer, j],
                 preferred_element_type=F32,
-            )
-            edge_weight[j] = weight.reshape(groups, rows, channels)
+            ).reshape(strips, groups, STRIP, channels)
+            gather_part(layer, j, 0, rows)
+
+    def rim_part(layer):
+        for j in range(pack):
+            gather_part(layer, j, rows, 2 * rim)
+
+    def gather_part(layer, j, first, count):
+        source = jnp.dot(
+            hot[j, :, :, :, first : first + count].reshape(groups * rows, count),
+            tables[layer, first : first + count],
+            preferred_element_type=F32,
+        )
+        product = edge_weight[j] * source.reshape(strips, groups, STRIP, channels)
+        total = jnp.sum(product, axis=1)
+        if first or j:
+            total = acc[...] + total
+        acc[...] = total
 
     @pl.when(g == 0)
     def _():
-        lane = lax.broadcasted_iota(jnp.int32, (rows, rows + 2 * rim), 1)
-        listing = jnp.concatenate(
-            [neighbours[...].astype(F32), jnp.zeros((BLOCK - slots, rows), F32)], axis=0
-        ).T.astype(jnp.int32)
-        for k in range(slots):
-            hot[k % pack, k // pack] = jnp.where(listing[:, k : k + 1] == lane, 1.0, 0.0).astype(BF16)
-        spread_r = (
-            lax.broadcasted_iota(jnp.int32, (channels, radial), 0) % radial
-            == lax.broadcasted_iota(jnp.int32, (channels, radial), 1)
-        ).astype(F32).astype(BF16)
-        spread_c = (
-            lax.broadcasted_iota(jnp.int32, (radial, channels), 1) % radial
-            == lax.broadcasted_iota(jnp.int32, (radial, channels), 0)
-        ).astype(F32).astype(BF16)
-        same_in = (
-            lax.broadcasted_iota(jnp.int32, (pack * basis, channels), 0) // basis
-            == lax.broadcasted_iota(jnp.int32, (pack * basis, channels), 1) // radial
-        )
-        same_mid = (
-            lax.broadcasted_iota(jnp.int32, (channels, channels), 0) // radial
-            == lax.broadcasted_iota(jnp.int32, (channels, channels), 1) // radial
-        )
-        for layer in range(layers):
-            flat = jnp.dot(radial_in[layer], spread_c, preferred_element_type=F32)
-            wide_in[layer] = jnp.where(
-                same_in, jnp.concatenate([flat] * pack, axis=0), 0.0
-            ).astype(BF16)
-            for m in range(2):
-                flat = jnp.dot(
-                    jnp.dot(spread_r, radial_mid[layer, m], preferred_element_type=F32).astype(
-                        BF16
-                    ),
-                    spread_c,
-                    preferred_element_type=F32,
-                )
-                wide_mid[layer, m] = jnp.where(same_mid, flat, 0.0).astype(BF16)
-            for j in range(pack):
-                wide_out[layer, j] = jnp.zeros((channels, channels), BF16)
-                wide_out[layer, j, j * radial : (j + 1) * radial, :] = radial_out[layer]
         for at, _, dist_sq, _, _, _ in edges():
             geometry[0, :, at] = jnp.sqrt(dist_sq)
-        radial_net(0)
+        radial_net()
 
     @pl.when(g == 1)
     def _():
@@ -385,6 +471,8 @@
 
     @pl.when(g == 0)
     def _():
+        for number in late[3:]:
+            load(number).wait()
         fx, fy, fz = out
         strength = jnp.sqrt(1.0 + fx * fx + fy * fy + fz * fz)
         site_result[2:3, :] = strength
@@ -395,35 +483,20 @@
             lifted = jnp.dot(
                 hidden_ref[...], node_in[layer], preferred_element_type=F32
             ).astype(BF16)
-            site = lax.broadcasted_iota(jnp.int32, (rows, rim), 0)
-            for side in range(2):
-                pick = jnp.where(site == send_rows[side : side + 1, :], 1.0, 0.0).astype(BF16)
-                lent[layer, side] = lax.dot_general(
-                    pick, lifted, (((0,), (0,)), ((), ())), preferred_element_type=F32
-                ).astype(BF16)
+            picked = jnp.dot(pick[...], lifted, preferred_element_type=F32).astype(BF16)
+            lent[layer] = picked.reshape(2, rim, channels)
             start(lift_copy, layer)
             tables[layer, 0:rows] = lifted
 
         for layer in range(layers):
             lift(layer)
-            edge_net(layer)
-            if layer + 1 < layers:
-                radial_net(layer + 1)
+            own_part(layer)
             arrive(lift_copy, layer)
-            acc[...] = jnp.zeros_like(acc)
-
-            @pl.loop(0, pack, unroll=2)
-            def _(j):
-                source = jnp.dot(
-                    hot[j].reshape(groups * rows, rows + 2 * rim),
-                    tables[layer],
-                    preferred_element_type=F32,
-                )
-                product = edge_weight[j] * source.reshape(groups, rows, channels)
-                acc[...] += jnp.sum(product, axis=0)
-
-            message = (acc[...] * (1.0 / slots)).astype(BF16)
-            update = silu(jnp.dot(message, node_out[layer], preferred_element_type=F32))
+            rim_part(layer)
+            message = (acc[...].reshape(rows, channels) * (1.0 / slots)).astype(BF16)
+            update = silu_of_half(
+                0.5 * jnp.dot(message, node_out[layer], preferred_element_type=F32)
+            )
             hidden_ref[...] = (hidden_ref[...].astype(F32) + update).astype(BF16)
 
         across = (((1,), (1,)), ((), ()))
@@ -537,16 +610,33 @@
     channels = features.shape[1]
     rim = send_rows.shape[1]
     pack = channels // radial
-    vmem = pl.BlockSpec(memory_space=pltpu.VMEM)
-    specs = [vmem] * 14
-    specs[6] = pl.BlockSpec(memory_space=pltpu.SMEM)
     dma = pltpu.SemaphoreType.DMA
+    operands = (
+        positions,
+        charges.reshape(1, -1),
+        polar.reshape(1, -1),
+        features,
+        neighbours.T,
+        send_rows,
+        blocks,
+        radial_in,
+        radial_mid,
+        radial_out,
+        node_in,
+        node_out,
+        field_gain.reshape(1, -1),
+        readout.T,
+    )
+    spaces = [pltpu.VMEM] * INPUTS
+    spaces[6] = pltpu.SMEM
     both = pl.pallas_call(
         functools.partial(kernel, n_dom, n_sub),
         out_shape=jax.ShapeDtypeStruct((2, 3, rows), F32),
-        in_specs=specs,
-        out_specs=vmem,
-        scratch_shapes=[
+        in_specs=[pl.BlockSpec(memory_space=pl.ANY)] * INPUTS,
+        out_specs=pl.BlockSpec(memory_space=pltpu.VMEM),
+        scratch_shapes=[space(a.shape, a.dtype) for space, a in zip(spaces, operands)]
+        + [
+            dma((INPUTS,)),
             pltpu.VMEM((own_blocks, 8, BLOCK), F32),
             pltpu.VMEM((n * own_blocks, 8, BLOCK), F32),
             pltpu.VMEM((8, listed * BLOCK), F32),
@@ -557,16 +647,19 @@
             pltpu.VMEM((1 + SWEEPS, 2, 8, rim), F32),
             pltpu.VMEM((1 + SWEEPS, 2, 8, rim), F32),
             pltpu.VMEM((5, slots, rows), F32),
-            pltpu.VMEM((pack, slots // pack, rows, rows + 2 * rim), BF16),
-            pltpu.VMEM((layers, slots // pack, rows, channels), BF16),
-            pltpu.VMEM((pack, slots // pack, rows, channels), F32),
+            pltpu.VMEM((pack, rows // STRIP, slots // pack, STRIP, rows + 2 * rim), BF16),
+            pltpu.VMEM((2 * rim, rows), BF16),
+            pltpu.VMEM((slots // pack * rows, pack * basis), BF16),
+            pltpu.VMEM((layers, 2, slots // pack * rows, channels), BF16),
+            pltpu.VMEM((layers, rows // STRIP, slots // pack, STRIP, channels), BF16),
+            pltpu.VMEM((pack, rows // STRIP, slots // pack, STRIP, channels), F32),
             pltpu.VMEM((layers, pack * basis, channels), BF16),
             pltpu.VMEM((layers, 2, channels, channels), BF16),
             pltpu.VMEM((layers, pack, channels, channels), BF16),
             pltpu.VMEM((layers, rows + 2 * rim, channels), BF16),
             pltpu.VMEM((layers, 2, rim, channels), BF16),
             pltpu.VMEM((rows, channels), BF16),
-            pltpu.VMEM((rows, channels), F32),
+            pltpu.VMEM((rows // STRIP, STRIP, channels), F32),
             pltpu.VMEM((3, rows), F32),
             pltpu.VMEM((3, rows), F32),
             pltpu.VMEM((3, listed * BLOCK), F32),
@@ -584,22 +677,7 @@
         compiler_params=pltpu.CompilerParams(
             collective_id=0, has_side_effects=True, vmem_limit_bytes=56 * 2**20
         ),
-    )(
-        positions,
-        charges.reshape(1, -1),
-        polar.reshape(1, -1),
-        features,
-        neighbours.T,
-        send_rows,
-        blocks,
-        radial_in,
-        radial_mid,
-        radial_out,
-        node_in,
-        node_out,
-        field_gain.reshape(1, -1),
-        readout.T,
-    )
+    )(*operands)
     return both[0], both[1]
 
 

time: 37 us -> 33 us (0.89)
  Pallas kernels: 34.9 us -> 30.8 us
    pallas_call x1, Pallas kernels: 34.9 us -> 30.8 us  [local(): pl.pallas_call(functools.partial(kernel, n_dom, n_sub), out_shape=jax.Sha...]
where the time goes in v1:
time: 33 us; the launch traced here: 32.7 us
  Pallas kernels  30.8 us (93%)
  local copies, waits for them, and re-layouts  1.28 us (4%)
  between operations  0.64 us (2%)
    pallas_call x1, Pallas kernels, local(): pl.pallas_call(functools.partial(kernel, n_dom, n_sub), out_shape=jax.Sha...  30.8 us
    squeeze x1, local copies, waits for them, and re-layouts, local(): return (both[0], both[1])  1.28 us

profile of v1, /device:TPU:1, one launch (start us, length us, event | category | flops | bytes accessed | tf_op | source)
XLA Modules:
  0.0 32.7 jit_solution(10538766284561193804)
XLA Ops:
  0.6 30.8 %shard_map.149 = f32[2,3,256]{2,1,0:T(4,128)} custom-call(f32[3,256]{1,0:T(4,128)} %refs_0_.1, f32[1,256]{1,0:T(1,128)} %bitcast.10, f32[1,256]{1,0:T(1,128)} %bitcast.11, bf16[256,256]{1,0:T(8,128)(2,1)} %refs_3_.1, s32[32,256]{1,0:T(8,128)} %bitcast.9, s32[2,128]{1,0:T(2,128)} %refs_5_.1, s32[4]{0:T(128)} %refs_6_.1, bf16[2,8,64]{2,1,0:T(8,128)(2,1)} %refs_7_.1, ...), custom_call_target="tpu_custom_call" | custom-call | tf_op jit(solution)/shard_map/pallas_call | solution.py:632
  31.4 1.3 %slice_bitcast_fusion = (f32[3,256]{1,0:T(4,128)}, f32[3,256]{1,0:T(4,128)}) fusion(f32[2,3,256]{2,1,0:T(4,128)} %shard_map.149), kind=kLoop, calls=%fused_computation | loop fusion | bytes 12288 | tf_op jit(solution)/shard_map/squeeze | solution.py:681

commit v2 on v1

--- a/solution.py
+++ b/solution.py
@@ -168,11 +168,11 @@
     own_rows[3:4, :] = charges[...]
     own = own_rows[...]
     for b in range(own_blocks):
-        packet[b] = own[:, b * BLOCK : (b + 1) * BLOCK]
+        packet[b] = own[0:4, b * BLOCK : (b + 1) * BLOCK]
 
     def fill_rims(step, values):
         for side in range(2):
-            index = jnp.broadcast_to(send_rows[side : side + 1, :], (8, rim))
+            index = jnp.broadcast_to(send_rows[side : side + 1, :], (4, rim))
             rim_out[step, side] = table_gather(
                 [(c, values[:, c * BLOCK : (c + 1) * BLOCK]) for c in range(own_blocks)],
                 index & (BLOCK - 1),
@@ -252,6 +252,8 @@
             pick[side * rim : (side + 1) * rim, :] = jnp.where(
                 lists[:, side : side + 1] == site, 1.0, 0.0
             ).astype(BF16)
+
+    def spread():
         for number in late[:3]:
             load(number).wait()
         spread_r = (
@@ -288,19 +290,19 @@
                 wide_out[layer, j] = jnp.zeros((channels, channels), BF16)
                 wide_out[layer, j, j * radial : (j + 1) * radial, :] = radial_out[layer]
 
-    fill_rims(0, own)
+    fill_rims(0, own[0:4])
 
     @pl.when(p == 0)
     def _():
         for step in range(1 + SWEEPS):
-            rim_in[step, 0] = jnp.zeros((8, rim), F32)
+            rim_in[step, 0] = jnp.zeros((4, rim), F32)
         for layer in range(layers):
             tables[layer, rows : rows + rim] = jnp.zeros((rim, channels), BF16)
 
     @pl.when(p == n - 1)
     def _():
         for step in range(1 + SWEEPS):
-            rim_in[step, 1] = jnp.zeros((8, rim), F32)
+            rim_in[step, 1] = jnp.zeros((4, rim), F32)
         for layer in range(layers):
             tables[layer, rows + rim :] = jnp.zeros((rim, channels), BF16)
 
@@ -322,9 +324,13 @@
 
     start(rim_copy, 0)
 
-    @pl.loop(0, n)
+    @pl.loop(0, n, unroll=4)
     def _(i):
         packet_copy(i).start()
+
+    @pl.when(g == 0)
+    def _():
+        spread()
 
     own_cols[...] = own.T
 
@@ -463,7 +469,9 @@
     for l in range(listed):
         tile = everyone[blocks[l]]
         near_rows[:, l * BLOCK : (l + 1) * BLOCK] = tile
-        near_cols[l * BLOCK : (l + 1) * BLOCK, :] = tile.T
+        near_cols[l * BLOCK : (l + 1) * BLOCK, :] = jnp.concatenate(
+            [tile, jnp.zeros_like(tile)], axis=0
+        ).T
 
     out = field(own, near_cols, listed * BLOCK, lambda at, source: source[:, 3:4], False)
     for c in range(3):
@@ -517,8 +525,7 @@
         dipole = [gain * outside[c : c + 1, :] for c in range(3)]
         for sweep in range(SWEEPS):
             step = 1 + sweep
-            stacked = jnp.concatenate(dipole + [jnp.zeros((5, rows), F32)], axis=0)
-            fill_rims(step, stacked)
+            fill_rims(step, jnp.concatenate(dipole + [jnp.zeros((1, rows), F32)], axis=0))
             start(rim_copy, step)
             arrive(rim_copy, step)
             fresh = [[], [], []]
@@ -550,7 +557,7 @@
         for sweep in range(SWEEPS):
             gone(rim_copy, 1 + sweep)
 
-    @pl.loop(0, n)
+    @pl.loop(0, n, unroll=4)
     def _(q):
         for b in range(own_blocks):
             total = jnp.zeros((3, BLOCK), F32)
@@ -570,7 +577,7 @@
             device_id_type=MESH,
         )
 
-    @pl.loop(0, n)
+    @pl.loop(0, n, unroll=4)
     def _(i):
         term_copy(i).start()
 
@@ -637,15 +644,15 @@
         scratch_shapes=[space(a.shape, a.dtype) for space, a in zip(spaces, operands)]
         + [
             dma((INPUTS,)),
-            pltpu.VMEM((own_blocks, 8, BLOCK), F32),
-            pltpu.VMEM((n * own_blocks, 8, BLOCK), F32),
-            pltpu.VMEM((8, listed * BLOCK), F32),
+            pltpu.VMEM((own_blocks, 4, BLOCK), F32),
+            pltpu.VMEM((n * own_blocks, 4, BLOCK), F32),
+            pltpu.VMEM((4, listed * BLOCK), F32),
             pltpu.VMEM((listed * BLOCK, 8), F32),
             pltpu.VMEM((8, rows), F32),
             pltpu.VMEM((rows, 8), F32),
             pltpu.VMEM((rows, 8), F32),
-            pltpu.VMEM((1 + SWEEPS, 2, 8, rim), F32),
-            pltpu.VMEM((1 + SWEEPS, 2, 8, rim), F32),
+            pltpu.VMEM((1 + SWEEPS, 2, 4, rim), F32),
+            pltpu.VMEM((1 + SWEEPS, 2, 4, rim), F32),
             pltpu.VMEM((5, slots, rows), F32),
             pltpu.VMEM((pack, rows // STRIP, slots // pack, STRIP, rows + 2 * rim), BF16),
             pltpu.VMEM((2 * rim, rows), BF16),
@@ -675,9 +682,9 @@
             dma(()),
         ],
         compiler_params=pltpu.CompilerParams(
-            collective_id=0, has_side_effects=True, vmem_limit_bytes=56 * 2**20
+            collective_id=0, has_side_effects=True, vmem_limit_bytes=40 * 2**20
         ),
-    )(*operands)
+    )(*(pltpu.with_memory_space_constraint(a, pltpu.HBM) for a in operands))
     return both[0], both[1]
 
 

time: 33 us -> 30.9 us (0.936)
  Pallas kernels: 30.8 us -> 29.5 us
  local copies, waits for them, and re-layouts: 1.28 us -> 0.6 us
    pallas_call x1, Pallas kernels: 30.8 us -> 29.5 us  [local(): pl.pallas_call(functools.partial(kernel, n_dom, n_sub), out_shape=jax.Sha...]
    squeeze x1, local copies, waits for them, and re-layouts: 1.28 us -> 0.6 us  [local(): return (both[0], both[1])]
where the time goes in v2:
time: 30.9 us; the launch traced here: 30.7 us
  Pallas kernels  29.5 us (95%)
  between operations  0.64 us (2%)
  local copies, waits for them, and re-layouts  0.6 us (2%)
    pallas_call x1, Pallas kernels, local(): pl.pallas_call(functools.partial(kernel, n_dom, n_sub), out_shape=jax.Sha...  29.5 us

profile of v2, /device:TPU:1, one launch (start us, length us, event | category | flops | bytes accessed | tf_op | source)
XLA Modules:
  0.0 30.7 jit_solution(4217534440791696619)
XLA Ops:
  0.6 29.5 %shard_map.149 = f32[2,3,256]{2,1,0:T(4,128)S(1)} custom-call(f32[3,256]{1,0:T(4,128)} %refs_0_.1, f32[1,256]{1,0:T(1,128)} %bitcast.10, f32[1,256]{1,0:T(1,128)} %bitcast.11, bf16[256,256]{1,0:T(8,128)(2,1)} %refs_3_.1, s32[32,256]{1,0:T(8,128)} %bitcast.9, s32[2,128]{1,0:T(2,128)} %refs_5_.1, s32[4]{0:T(128)} %refs_6_.1, bf16[2,8,64]{2,1,0:T(8,128)(2,1)} %refs_7_.1, ...), custom_call_target="tpu_custom_call" | custom-call | tf_op jit(solution)/shard_map/pallas_call | solution.py:639
  30.1 0.6 %slice_bitcast_fusion = (f32[3,256]{1,0:T(4,128)}, f32[3,256]{1,0:T(4,128)}) fusion(f32[2,3,256]{2,1,0:T(4,128)S(1)} %shard_map.149), kind=kLoop, calls=%fused_computation | loop fusion | bytes 12288 | tf_op jit(solution)/shard_map/squeeze | solution.py:688

commit v3 on v2

--- a/solution.py
+++ b/solution.py
@@ -29,8 +29,9 @@
     )
 
 
-def table_gather(pieces, local, chunk):
-    total = jnp.zeros(local.shape, F32)
+def table_gather(pieces, local, chunk, total=None):
+    if total is None:
+        total = jnp.zeros(local.shape, F32)
     for number, rows in pieces:
         total = jnp.where(chunk == number, lane_pick(rows, local), total)
     return total
@@ -80,6 +81,8 @@
     wide_out,
     tables,
     lent,
+    lent_cols,
+    reach,
     hidden_ref,
     acc,
     outside,
@@ -129,9 +132,13 @@
     )
     early = (0, 1, 2, 4, 5, 6)
     late = (7, 8, 9, 3, 10, 11, 12, 13)
+    spread_needs = 4
 
     def load(number):
-        return pltpu.make_async_copy(sources[number], held[number], in_sem.at[number])
+        target = held[number]
+        if number == 3:
+            target = target.at[pl.ds(0, rows)]
+        return pltpu.make_async_copy(sources[number], target, in_sem.at[number])
 
     for number in early:
         load(number).start()
@@ -195,9 +202,10 @@
         )
 
     def lift_copy(layer, side, q):
+        target = tables.at[layer] if layer else features
         return side_copy(
             lent.at[layer, side],
-            tables.at[layer, pl.ds(rows + side * rim, rim)],
+            target.at[pl.ds(rows + side * rim, rim)],
             lift_send,
             lift_recv,
             layer,
@@ -254,7 +262,7 @@
             ).astype(BF16)
 
     def spread():
-        for number in late[:3]:
+        for number in late[:spread_needs]:
             load(number).wait()
         spread_r = (
             lax.broadcasted_iota(jnp.int32, (channels, radial), 0) % radial
@@ -290,20 +298,35 @@
                 wide_out[layer, j] = jnp.zeros((channels, channels), BF16)
                 wide_out[layer, j, j * radial : (j + 1) * radial, :] = radial_out[layer]
 
+    def lend(layer, values):
+        picked = jnp.dot(pick[...], values, preferred_element_type=F32).astype(BF16)
+        lent[layer] = picked.reshape(2, rim, channels)
+
     fill_rims(0, own[0:4])
+
+    @pl.when(g == 0)
+    def _():
+        spot = lax.broadcasted_iota(jnp.int32, (1, rim), 1)
+        names = jnp.zeros((1, rim), F32)
+        for l in range(listed):
+            names = jnp.where(spot == l, blocks[l].astype(F32), names)
+        for side in range(2):
+            rim_out[0, side, 3:4, :] = names
 
     @pl.when(p == 0)
     def _():
         for step in range(1 + SWEEPS):
             rim_in[step, 0] = jnp.zeros((4, rim), F32)
-        for layer in range(layers):
+        features[rows : rows + rim] = jnp.zeros((rim, channels), BF16)
+        for layer in range(1, layers):
             tables[layer, rows : rows + rim] = jnp.zeros((rim, channels), BF16)
 
     @pl.when(p == n - 1)
     def _():
         for step in range(1 + SWEEPS):
             rim_in[step, 1] = jnp.zeros((4, rim), F32)
-        for layer in range(layers):
+        features[rows + rim :] = jnp.zeros((rim, channels), BF16)
+        for layer in range(1, layers):
             tables[layer, rows + rim :] = jnp.zeros((rim, channels), BF16)
 
     @pl.when(g == 0)
@@ -331,40 +354,61 @@
     @pl.when(g == 0)
     def _():
         spread()
+        lend(0, features[0:rows])
 
     own_cols[...] = own.T
 
-    def field(targets, source_cols, count, charge, dipole):
+    def field(targets, source_cols, count):
         x, y, z = (targets[c : c + 1, :] for c in range(3))
-        width = targets.shape[1]
 
         def step(i, sums):
-            at = pl.ds(pl.multiple_of(i * 8, 8), 8)
-            source = source_cols[at, :]
+            source = source_cols[pl.ds(pl.multiple_of(i * 8, 8), 8), :]
             rx = x - source[:, 0:1]
             ry = y - source[:, 1:2]
             rz = z - source[:, 2:3]
             w = lax.rsqrt(rx * rx + ry * ry + rz * rz + SMOOTH)
+            s = source[:, 3:4] * (w * w * w)
+            return (sums[0] + rx * s, sums[1] + ry * s, sums[2] + rz * s)
+
+        zero = jnp.zeros((8, targets.shape[1]), F32)
+        sums = lax.fori_loop(0, count // 8, step, (zero, zero, zero), unroll=True)
+        return [jnp.sum(s, axis=0, keepdims=True) for s in sums]
+
+    def term_geometry(dipole):
+        x, y, z = (near_rows[c : c + 1, :] for c in range(3))
+
+        @pl.loop(0, rows // 8, unroll=8)
+        def _(i):
+            at = pl.ds(pl.multiple_of(i * 8, 8), 8)
+            source = own_cols[at, :]
+            r = (x - source[:, 0:1], y - source[:, 1:2], z - source[:, 2:3])
+            w = lax.rsqrt(r[0] * r[0] + r[1] * r[1] + r[2] * r[2] + SMOOTH)
             w2 = w * w
             w3 = w2 * w
+            for c in range(3):
+                reach[c, at, :] = r[c] if dipole else r[c] * w3
+            if dipole:
+                reach[3, at, :] = w3
+                reach[4, at, :] = 3.0 * (w3 * w2)
+
+    def send_terms(dipole):
+        def step(i, sums):
+            at = pl.ds(pl.multiple_of(i * 8, 8), 8)
+            d = extra_cols[at, :]
+            r = [reach[c, at, :] for c in range(3)]
             if not dipole:
-                s = charge(at, source) * w3
-                return (sums[0] + rx * s, sums[1] + ry * s, sums[2] + rz * s)
-            d = extra_cols[at, :]
-            dx, dy, dz = d[:, 0:1], d[:, 1:2], d[:, 2:3]
-            s = 3.0 * (rx * dx + ry * dy + rz * dz) * (w3 * w2)
-            return (
-                sums[0] + (rx * s - dx * w3),
-                sums[1] + (ry * s - dy * w3),
-                sums[2] + (rz * s - dz * w3),
-            )
-
-        zero = jnp.zeros((8, width), F32)
-        sums = lax.fori_loop(0, count // 8, step, (zero, zero, zero), unroll=16)
-        return [jnp.sum(s, axis=0, keepdims=True) for s in sums]
+                return tuple(sums[c] + r[c] * d[:, 0:1] for c in range(3))
+            w3 = reach[3, at, :]
+            d = [d[:, c : c + 1] for c in range(3)]
+            s = (r[0] * d[0] + r[1] * d[1] + r[2] * d[2]) * reach[4, at, :]
+            return tuple(sums[c] + (r[c] * s - d[c] * w3) for c in range(3))
+
+        zero = jnp.zeros((8, listed * BLOCK), F32)
+        sums = lax.fori_loop(0, rows // 8, step, (zero, zero, zero), unroll=True)
+        for c in range(3):
+            terms[c : c + 1, :] = jnp.sum(sums[c], axis=0, keepdims=True)
 
     def edges():
-        arrive(rim_copy, 0)
         for tile in range(own_blocks):
             at = slice(tile * BLOCK, (tile + 1) * BLOCK)
             index = neighbours[:, at]
@@ -381,20 +425,9 @@
             dist_sq = ox * ox + oy * oy + oz * oz + SMOOTH
             yield at, (ox, oy, oz), dist_sq, picked[3], local, chunk
 
-    def send_terms(charge, dipole):
-        width = listed * BLOCK
-        for half in range(0, width, 2 * BLOCK):
-            out = field(
-                near_rows[:, half : half + 2 * BLOCK], own_cols, rows, charge, dipole
-            )
-            for c in range(3):
-                terms[c : c + 1, half : half + 2 * BLOCK] = out[c]
-
     centre = lax.broadcasted_iota(jnp.int32, (basis, rows), 0).astype(F32) * SPACING
 
-    def radial_net():
-        half = groups // 2
-        spans = [range(half), range(half, groups)]
+    def waves():
         for q in range(groups):
             parts = []
             for j in range(pack):
@@ -403,25 +436,29 @@
                 parts.append(jnp.exp(-(away * away)))
             turned = jnp.concatenate(parts, axis=0).T
             wave[q * rows : (q + 1) * rows, :] = turned.astype(BF16)
-        for layer in range(layers):
-            for step in range(3):
-                for part, span in enumerate(spans):
-                    at = slice(span[0] * rows, (span[-1] + 1) * rows)
-                    if step == 0:
-                        source, weight = wave[at, :], wide_in[layer]
-                    else:
-                        source, weight = stage[layer, step - 1, at, :], wide_mid[layer, step - 1]
-                    h = silu_of_half(jnp.dot(source, weight, preferred_element_type=F32)).astype(BF16)
-                    if step < 2:
-                        stage[layer, step, at, :] = h
-                    else:
-                        for i, q in enumerate(span):
-                            third[layer, :, q] = h[i * rows : (i + 1) * rows].reshape(
-                                strips, STRIP, channels
-                            )
-
-    def own_part(layer):
+
+    def radial_net(layer):
+        half = groups // 2
+        spans = [range(half), range(half, groups)]
+        for step in range(3):
+            for part, span in enumerate(spans):
+                at = slice(span[0] * rows, (span[-1] + 1) * rows)
+                if step == 0:
+                    source, weight = wave[at, :], wide_in[layer]
+                else:
+                    source, weight = stage[step - 1, at, :], wide_mid[layer, step - 1]
+                h = silu_of_half(jnp.dot(source, weight, preferred_element_type=F32)).astype(BF16)
+                if step < 2:
+                    stage[step, at, :] = h
+                else:
+                    for i, q in enumerate(span):
+                        third[layer, :, q] = h[i * rows : (i + 1) * rows].reshape(
+                            strips, STRIP, channels
+                        )
+
+    def own_part(layer, beside):
         for j in range(pack):
+            beside(j)
             edge_weight[j] = jnp.dot(
                 third[layer].reshape(groups * rows, channels),
                 wide_out[layer, j],
@@ -447,12 +484,16 @@
 
     @pl.when(g == 0)
     def _():
+        arrive(rim_copy, 0)
+        start(lift_copy, 0)
         for at, _, dist_sq, _, _, _ in edges():
             geometry[0, :, at] = jnp.sqrt(dist_sq)
-        radial_net()
+        waves()
+        radial_net(0)
 
     @pl.when(g == 1)
     def _():
+        arrive(rim_copy, 0)
         for at, offset, dist_sq, source_charge, _, _ in edges():
             w = lax.rsqrt(dist_sq)
             w2 = w * w
@@ -473,33 +514,87 @@
             [tile, jnp.zeros_like(tile)], axis=0
         ).T
 
-    out = field(own, near_cols, listed * BLOCK, lambda at, source: source[:, 3:4], False)
-    for c in range(3):
-        outside[c : c + 1, :] = out[c]
+    def lent_near():
+        names = [
+            [jnp.broadcast_to(rim_in[0, side, 3:4, l : l + 1], (4, BLOCK)) for l in range(listed)]
+            for side in range(2)
+        ]
+
+        def step(b, found):
+            tile = everyone[b]
+            return tuple(
+                tuple(
+                    jnp.where(names[side][l] == b.astype(F32), tile, found[side][l])
+                    for l in range(listed)
+                )
+                for side in range(2)
+            )
+
+        blank = jnp.zeros((4, BLOCK), F32)
+        found = lax.fori_loop(
+            0, n * own_blocks, step, ((blank,) * listed,) * 2, unroll=max(8, min(32, n * own_blocks))
+        )
+        for side in range(2):
+            for l in range(listed):
+                lent_cols[side, l * BLOCK : (l + 1) * BLOCK, :] = jnp.concatenate(
+                    [found[side][l], blank], axis=0
+                ).T
 
     @pl.when(g == 0)
     def _():
-        for number in late[3:]:
+        for number in late[spread_needs:]:
             load(number).wait()
-        fx, fy, fz = out
-        strength = jnp.sqrt(1.0 + fx * fx + fy * fy + fz * fz)
+
+        def strength_of(fields):
+            fx, fy, fz = fields
+            return jnp.sqrt(1.0 + fx * fx + fy * fy + fz * fz)
+
+        def embed(strength, at):
+            column = jnp.broadcast_to(strength, (8, strength.shape[1])).T[:, 0:1]
+            return (features[at].astype(F32) + column * field_gain[...]).astype(BF16)
+
+        def lent_field(side):
+            return field(rim_in[0, side], lent_cols.at[side], listed * BLOCK)
+
+        strength = strength_of(field(own, near_cols, listed * BLOCK))
         site_result[2:3, :] = strength
-        strength_col = jnp.broadcast_to(strength, (8, rows)).T[:, 0:1]
-        hidden_ref[...] = (features[...].astype(F32) + strength_col * field_gain[...]).astype(BF16)
+        hidden_ref[...] = embed(strength, slice(0, rows))
+        tables[0, 0:rows] = jnp.dot(
+            hidden_ref[...], node_in[0], preferred_element_type=F32
+        ).astype(BF16)
+        fields = []
+
+        def lent_lift(j):
+            if j == 0:
+                lent_near()
+            if j < 2:
+                fields.append(lent_field(j))
+            if j == pack - 1:
+                arrive(lift_copy, 0)
+                ends = (p > 0, p < n - 1)
+                for side in range(2):
+                    at = slice(rows + side * rim, rows + (side + 1) * rim)
+                    hidden = embed(strength_of(fields[side]), at)
+                    lifted = jnp.dot(hidden, node_in[0], preferred_element_type=F32)
+                    tables[0, at] = jnp.where(ends[side], lifted, 0.0).astype(BF16)
 
         def lift(layer):
             lifted = jnp.dot(
                 hidden_ref[...], node_in[layer], preferred_element_type=F32
             ).astype(BF16)
-            picked = jnp.dot(pick[...], lifted, preferred_element_type=F32).astype(BF16)
-            lent[layer] = picked.reshape(2, rim, channels)
+            lend(layer, lifted)
             start(lift_copy, layer)
             tables[layer, 0:rows] = lifted
 
         for layer in range(layers):
-            lift(layer)
-            own_part(layer)
-            arrive(lift_copy, layer)
+            if layer:
+                lift(layer)
+                radial_net(layer)
+            own_part(layer, (lambda j: None) if layer else lent_lift)
+            if layer == layers - 1:
+                term_geometry(False)
+            if layer:
+                arrive(lift_copy, layer)
             rim_part(layer)
             message = (acc[...].reshape(rows, channels) * (1.0 / slots)).astype(BF16)
             update = silu_of_half(
@@ -514,12 +609,15 @@
         site_result[0:2, :] = lax.dot_general(
             readout[...], hidden_ref[...], across, preferred_element_type=F32
         )
-        send_terms(lambda at, source: extra_cols[at, 0:1], False)
+        send_terms(False)
         for layer in range(layers):
             gone(lift_copy, layer)
 
     @pl.when(g == 1)
     def _():
+        out = field(own, near_cols, listed * BLOCK)
+        for c in range(3):
+            outside[c : c + 1, :] = out[c]
         gain = polar[...]
         outside[...] = outside[...] + pairs[...]
         dipole = [gain * outside[c : c + 1, :] for c in range(3)]
@@ -527,6 +625,21 @@
             step = 1 + sweep
             fill_rims(step, jnp.concatenate(dipole + [jnp.zeros((1, rows), F32)], axis=0))
             start(rim_copy, step)
+            near_part = []
+            for tile in range(own_blocks):
+                index = neighbours[:, tile * BLOCK : (tile + 1) * BLOCK]
+                local = index & (BLOCK - 1)
+                chunk = lax.shift_right_logical(index, 7)
+                near_part.append([
+                    table_gather(
+                        [(b, dipole[c][:, b * BLOCK : (b + 1) * BLOCK]) for b in range(own_blocks)],
+                        local,
+                        chunk,
+                    )
+                    for c in range(3)
+                ])
+            if sweep == 0:
+                term_geometry(True)
             arrive(rim_copy, step)
             fresh = [[], [], []]
             for tile in range(own_blocks):
@@ -534,14 +647,15 @@
                 index = neighbours[:, at]
                 local = index & (BLOCK - 1)
                 chunk = lax.shift_right_logical(index, 7)
-                d = []
-                for c in range(3):
-                    pieces = [
-                        (b, dipole[c][:, b * BLOCK : (b + 1) * BLOCK]) for b in range(own_blocks)
-                    ] + [
-                        (own_blocks + side, rim_in[step, side, c : c + 1, :]) for side in range(2)
-                    ]
-                    d.append(table_gather(pieces, local, chunk))
+                d = [
+                    table_gather(
+                        [(own_blocks + side, rim_in[step, side, c : c + 1, :]) for side in range(2)],
+                        local,
+                        chunk,
+                        near_part[tile][c],
+                    )
+                    for c in range(3)
+                ]
                 r = [geometry[c, :, at] for c in range(3)]
                 w3 = geometry[3, :, at]
                 s = (r[0] * d[0] + r[1] * d[1] + r[2] * d[2]) * geometry[4, :, at]
@@ -553,7 +667,7 @@
             site_result[c : c + 1, :] = dipole[c]
         stacked = jnp.concatenate(dipole + [jnp.zeros((5, rows), F32)], axis=0)
         extra_cols[...] = stacked.T
-        send_terms(None, True)
+        send_terms(True)
         for sweep in range(SWEEPS):
             gone(rim_copy, 1 + sweep)
 
@@ -636,12 +750,14 @@
     )
     spaces = [pltpu.VMEM] * INPUTS
     spaces[6] = pltpu.SMEM
+    shapes = [a.shape for a in operands]
+    shapes[3] = (rows + 2 * rim, channels)
     both = pl.pallas_call(
         functools.partial(kernel, n_dom, n_sub),
         out_shape=jax.ShapeDtypeStruct((2, 3, rows), F32),
         in_specs=[pl.BlockSpec(memory_space=pl.ANY)] * INPUTS,
         out_specs=pl.BlockSpec(memory_space=pltpu.VMEM),
-        scratch_shapes=[space(a.shape, a.dtype) for space, a in zip(spaces, operands)]
+        scratch_shapes=[space(shape, a.dtype) for space, shape, a in zip(spaces, shapes, operands)]
         + [
             dma((INPUTS,)),
             pltpu.VMEM((own_blocks, 4, BLOCK), F32),
@@ -657,7 +773,7 @@
             pltpu.VMEM((pack, rows // STRIP, slots // pack, STRIP, rows + 2 * rim), BF16),
             pltpu.VMEM((2 * rim, rows), BF16),
             pltpu.VMEM((slots // pack * rows, pack * basis), BF16),
-            pltpu.VMEM((layers, 2, slots // pack * rows, channels), BF16),
+            pltpu.VMEM((2, slots // pack * rows, channels), BF16),
             pltpu.VMEM((layers, rows // STRIP, slots // pack, STRIP, channels), BF16),
             pltpu.VMEM((pack, rows // STRIP, slots // pack, STRIP, channels), F32),
             pltpu.VMEM((layers, pack * basis, channels), BF16),
@@ -665,6 +781,8 @@
             pltpu.VMEM((layers, pack, channels, channels), BF16),
             pltpu.VMEM((layers, rows + 2 * rim, channels), BF16),
             pltpu.VMEM((layers, 2, rim, channels), BF16),
+            pltpu.VMEM((2, listed * BLOCK, 8), F32),
+            pltpu.VMEM((5, rows, listed * BLOCK), F32),
             pltpu.VMEM((rows, channels), BF16),
             pltpu.VMEM((rows // STRIP, STRIP, channels), F32),
             pltpu.VMEM((3, rows), F32),

time: 30.9 us -> 29.7 us (0.961)
  the two profiles are of different devices: /device:TPU:1 before, /device:TPU:0 now
where the time goes in v3:
time: 29.7 us; the launch traced here: 29.6 us
  Pallas kernels  28.3 us (95%)
  between operations  0.64 us (2%)
  local copies, waits for them, and re-layouts  0.6 us (2%)
    pallas_call x1, Pallas kernels, local(): pl.pallas_call(functools.partial(kernel, n_dom, n_sub), out_shape=jax.Sha...  28.3 us
    squeeze x1, local copies, waits for them, and re-layouts, local(): return (both[0], both[1])  0.6 us

profile of v3, /device:TPU:0, one launch (start us, length us, event | category | flops | bytes accessed | tf_op | source)
XLA Modules:
  0.0 29.6 jit_solution(2723441451465545051)
XLA Ops:
  0.6 28.3 %shard_map.149 = f32[2,3,256]{2,1,0:T(4,128)S(1)} custom-call(f32[3,256]{1,0:T(4,128)} %refs_0_.1, f32[1,256]{1,0:T(1,128)} %bitcast.10, f32[1,256]{1,0:T(1,128)} %bitcast.11, bf16[256,256]{1,0:T(8,128)(2,1)} %refs_3_.1, s32[32,256]{1,0:T(8,128)} %bitcast.9, s32[2,128]{1,0:T(2,128)} %refs_5_.1, s32[4]{0:T(128)} %refs_6_.1, bf16[2,8,64]{2,1,0:T(8,128)(2,1)} %refs_7_.1, ...), custom_call_target="tpu_custom_call" | custom-call | tf_op jit(solution)/shard_map/pallas_call | solution.py:755
  29.0 0.6 %slice_bitcast_fusion = (f32[3,256]{1,0:T(4,128)}, f32[3,256]{1,0:T(4,128)}) fusion(f32[2,3,256]{2,1,0:T(4,128)S(1)} %shard_map.149), kind=kLoop, calls=%fused_computation | loop fusion | bytes 12288 | tf_op jit(solution)/shard_map/squeeze | solution.py:806

commit v4 on v3

--- a/solution.py
+++ b/solution.py
@@ -14,6 +14,7 @@
 MESH = pl.DeviceIdType.MESH
 INPUTS = 14
 STRIP = 16
+EARLY = 2
 F32 = jnp.float32
 BF16 = jnp.bfloat16
 
@@ -147,7 +148,13 @@
         return (group, lax.div(q, n_sub), lax.rem(q, n_sub))
 
     def peer(i):
-        return lax.rem(p + i, n)
+        if n % 4:
+            return lax.rem(p + i, n)
+        quarter = n // 4
+        second = lax.div(2 * p, n)
+        turn = lax.div(i, quarter)
+        far = second * turn + (1 - second) * (3 - turn)
+        return far * quarter + lax.rem(p + i, quarter)
 
     barrier = pltpu.get_barrier_semaphore()
 
@@ -374,12 +381,10 @@
         sums = lax.fori_loop(0, count // 8, step, (zero, zero, zero), unroll=True)
         return [jnp.sum(s, axis=0, keepdims=True) for s in sums]
 
-    def term_geometry(dipole):
+    def term_geometry(dipole, part, parts):
         x, y, z = (near_rows[c : c + 1, :] for c in range(3))
-
-        @pl.loop(0, rows // 8, unroll=8)
-        def _(i):
-            at = pl.ds(pl.multiple_of(i * 8, 8), 8)
+        for i in range(part * rows // 8 // parts, (part + 1) * rows // 8 // parts):
+            at = slice(i * 8, i * 8 + 8)
             source = own_cols[at, :]
             r = (x - source[:, 0:1], y - source[:, 1:2], z - source[:, 2:3])
             w = lax.rsqrt(r[0] * r[0] + r[1] * r[1] + r[2] * r[2] + SMOOTH)
@@ -456,14 +461,18 @@
                             strips, STRIP, channels
                         )
 
+    def edge_part(layer, j):
+        edge_weight[j] = jnp.dot(
+            third[layer].reshape(groups * rows, channels),
+            wide_out[layer, j],
+            preferred_element_type=F32,
+        ).reshape(strips, groups, STRIP, channels)
+
     def own_part(layer, beside):
         for j in range(pack):
             beside(j)
-            edge_weight[j] = jnp.dot(
-                third[layer].reshape(groups * rows, channels),
-                wide_out[layer, j],
-                preferred_element_type=F32,
-            ).reshape(strips, groups, STRIP, channels)
+            if layer or j >= EARLY:
+                edge_part(layer, j)
             gather_part(layer, j, 0, rows)
 
     def rim_part(layer):
@@ -490,6 +499,8 @@
             geometry[0, :, at] = jnp.sqrt(dist_sq)
         waves()
         radial_net(0)
+        for j in range(EARLY):
+            edge_part(0, j)
 
     @pl.when(g == 1)
     def _():
@@ -549,8 +560,10 @@
             fx, fy, fz = fields
             return jnp.sqrt(1.0 + fx * fx + fy * fy + fz * fz)
 
-        def embed(strength, at):
-            column = jnp.broadcast_to(strength, (8, strength.shape[1])).T[:, 0:1]
+        def column_of(strength):
+            return jnp.broadcast_to(strength, (8, strength.shape[1])).T[:, 0:1]
+
+        def embed(column, at):
             return (features[at].astype(F32) + column * field_gain[...]).astype(BF16)
 
         def lent_field(side):
@@ -558,23 +571,25 @@
 
         strength = strength_of(field(own, near_cols, listed * BLOCK))
         site_result[2:3, :] = strength
-        hidden_ref[...] = embed(strength, slice(0, rows))
+        hidden_ref[...] = embed(column_of(strength), slice(0, rows))
         tables[0, 0:rows] = jnp.dot(
             hidden_ref[...], node_in[0], preferred_element_type=F32
         ).astype(BF16)
-        fields = []
+        fields, columns = [], []
 
         def lent_lift(j):
             if j == 0:
                 lent_near()
             if j < 2:
                 fields.append(lent_field(j))
+            if j == 2:
+                columns.extend(column_of(strength_of(part)) for part in fields)
             if j == pack - 1:
                 arrive(lift_copy, 0)
                 ends = (p > 0, p < n - 1)
                 for side in range(2):
                     at = slice(rows + side * rim, rows + (side + 1) * rim)
-                    hidden = embed(strength_of(fields[side]), at)
+                    hidden = embed(columns[side], at)
                     lifted = jnp.dot(hidden, node_in[0], preferred_element_type=F32)
                     tables[0, at] = jnp.where(ends[side], lifted, 0.0).astype(BF16)
 
@@ -587,12 +602,14 @@
             tables[layer, 0:rows] = lifted
 
         for layer in range(layers):
+            def beside(j, layer=layer):
+                if layer == layers - 1:
+                    term_geometry(False, j, pack)
+
             if layer:
                 lift(layer)
                 radial_net(layer)
-            own_part(layer, (lambda j: None) if layer else lent_lift)
-            if layer == layers - 1:
-                term_geometry(False)
+            own_part(layer, beside if layer else lent_lift)
             if layer:
                 arrive(lift_copy, layer)
             rim_part(layer)
@@ -639,7 +656,7 @@
                     for c in range(3)
                 ])
             if sweep == 0:
-                term_geometry(True)
+                term_geometry(True, 0, 1)
             arrive(rim_copy, step)
             fresh = [[], [], []]
             for tile in range(own_blocks):
@@ -671,7 +688,7 @@
         for sweep in range(SWEEPS):
             gone(rim_copy, 1 + sweep)
 
-    @pl.loop(0, n, unroll=4)
+    @pl.loop(0, n, unroll=min(n, 16))
     def _(q):
         for b in range(own_blocks):
             total = jnp.zeros((3, BLOCK), F32)

time: 29.7 us -> 29.7 us (level)
  no operation moved by 1% of the time
where the time goes in v4:
time: 29.7 us; the launch traced here: 29.5 us
  Pallas kernels  28.3 us (95%)
  between operations  0.64 us (2%)
  local copies, waits for them, and re-layouts  0.6 us (2%)
    pallas_call x1, Pallas kernels, local(): pl.pallas_call(functools.partial(kernel, n_dom, n_sub), out_shape=jax.Sha...  28.3 us
    squeeze x1, local copies, waits for them, and re-layouts, local(): return (both[0], both[1])  0.6 us

profile of v4, /device:TPU:0, one launch (start us, length us, event | category | flops | bytes accessed | tf_op | source)
XLA Modules:
  0.0 29.5 jit_solution(10056206473563442348)
XLA Ops:
  0.6 28.3 %shard_map.149 = f32[2,3,256]{2,1,0:T(4,128)S(1)} custom-call(f32[3,256]{1,0:T(4,128)} %refs_0_.1, f32[1,256]{1,0:T(1,128)} %bitcast.10, f32[1,256]{1,0:T(1,128)} %bitcast.11, bf16[256,256]{1,0:T(8,128)(2,1)} %refs_3_.1, s32[32,256]{1,0:T(8,128)} %bitcast.9, s32[2,128]{1,0:T(2,128)} %refs_5_.1, s32[4]{0:T(128)} %refs_6_.1, bf16[2,8,64]{2,1,0:T(8,128)(2,1)} %refs_7_.1, ...), custom_call_target="tpu_custom_call" | custom-call | tf_op jit(solution)/shard_map/pallas_call | solution.py:772
  28.9 0.6 %slice_bitcast_fusion = (f32[3,256]{1,0:T(4,128)}, f32[3,256]{1,0:T(4,128)}) fusion(f32[2,3,256]{2,1,0:T(4,128)S(1)} %shard_map.149), kind=kLoop, calls=%fused_computation | loop fusion | bytes 12288 | tf_op jit(solution)/shard_map/squeeze | solution.py:823

commit v5 on v4

--- a/solution.py
+++ b/solution.py
@@ -8,6 +8,7 @@
 from jax.sharding import PartitionSpec as P
 
 SWEEPS = 4
+ROUNDS = SWEEPS // 2
 BLOCK = 128
 SMOOTH = 1.0
 SPACING = 0.75
@@ -32,7 +33,7 @@
 
 def table_gather(pieces, local, chunk, total=None):
     if total is None:
-        total = jnp.zeros(local.shape, F32)
+        total = jnp.zeros(local.shape, pieces[0][1].dtype)
     for number, rows in pieces:
         total = jnp.where(chunk == number, lane_pick(rows, local), total)
     return total
@@ -70,6 +71,13 @@
     extra_cols,
     rim_out,
     rim_in,
+    flat_out,
+    flat_in,
+    far_in,
+    lists_out,
+    lists_in,
+    fixed_out,
+    fixed_in,
     geometry,
     hot,
     pick,
@@ -99,6 +107,14 @@
     lift_recv,
     term_send,
     term_recv,
+    flat_send,
+    flat_recv,
+    far_send,
+    far_recv,
+    list_send,
+    list_recv,
+    fixed_send,
+    fixed_recv,
     ) = refs[INPUTS:]
     g = lax.axis_index("grp")
     p = lax.axis_index("dom") * n_sub + lax.axis_index("sub")
@@ -170,6 +186,14 @@
     def _():
         pl.semaphore_signal(barrier, inc=1, device_id=place(g, p + 1), device_id_type=MESH)
 
+    @pl.when(p > 1)
+    def _():
+        pl.semaphore_signal(barrier, inc=1, device_id=place(g, p - 2), device_id_type=MESH)
+
+    @pl.when(p < n - 2)
+    def _():
+        pl.semaphore_signal(barrier, inc=1, device_id=place(g, p + 2), device_id_type=MESH)
+
     @pl.when(g == 0)
     def _():
         for number in late:
@@ -184,14 +208,17 @@
     for b in range(own_blocks):
         packet[b] = own[0:4, b * BLOCK : (b + 1) * BLOCK]
 
-    def fill_rims(step, values):
+    def fill(target, values):
         for side in range(2):
-            index = jnp.broadcast_to(send_rows[side : side + 1, :], (4, rim))
-            rim_out[step, side] = table_gather(
+            index = jnp.broadcast_to(send_rows[side : side + 1, :], (values.shape[0], rim))
+            target[side] = table_gather(
                 [(c, values[:, c * BLOCK : (c + 1) * BLOCK]) for c in range(own_blocks)],
                 index & (BLOCK - 1),
                 lax.shift_right_logical(index, 7),
             )
+
+    def fill_rims(step, values):
+        fill(rim_out.at[step], values)
 
     def side_copy(src, dst, send, recv, step, side, q):
         return pltpu.make_async_remote_copy(
@@ -220,32 +247,52 @@
             q,
         )
 
-    def start(copy, step):
-        @pl.when(p < n - 1)
+    def flat_copy(step, side, q):
+        return side_copy(
+            flat_out.at[step], flat_in.at[step, side], flat_send, flat_recv, step, side, q
+        )
+
+    def far_copy(step, side, q):
+        return side_copy(
+            rim_out.at[step, side], far_in.at[step, side], far_send, far_recv, step, side, q
+        )
+
+    def list_copy(step, side, q):
+        return side_copy(
+            lists_out.at[side], lists_in.at[side], list_send, list_recv, step, side, q
+        )
+
+    def fixed_copy(step, side, q):
+        return side_copy(
+            fixed_out.at[side], fixed_in.at[side], fixed_send, fixed_recv, step, side, q
+        )
+
+    def start(copy, step, away=1):
+        @pl.when(p < n - away)
         def _():
-            copy(step, 0, p + 1).start()
-
-        @pl.when(p > 0)
+            copy(step, 0, p + away).start()
+
+        @pl.when(p > away - 1)
         def _():
-            copy(step, 1, p - 1).start()
-
-    def arrive(copy, step):
-        @pl.when(p > 0)
+            copy(step, 1, p - away).start()
+
+    def arrive(copy, step, away=1):
+        @pl.when(p > away - 1)
         def _():
-            copy(step, 0, p - 1).wait_recv()
-
-        @pl.when(p < n - 1)
+            copy(step, 0, p - away).wait_recv()
+
+        @pl.when(p < n - away)
         def _():
-            copy(step, 1, p + 1).wait_recv()
-
-    def gone(copy, step):
-        @pl.when(p < n - 1)
+            copy(step, 1, p + away).wait_recv()
+
+    def gone(copy, step, away=1):
+        @pl.when(p < n - away)
         def _():
-            copy(step, 0, p + 1).wait_send()
-
-        @pl.when(p > 0)
+            copy(step, 0, p + away).wait_send()
+
+        @pl.when(p > away - 1)
         def _():
-            copy(step, 1, p - 1).wait_send()
+            copy(step, 1, p - away).wait_send()
 
     def prepare():
         width = rows + 2 * rim
@@ -322,7 +369,7 @@
 
     @pl.when(p == 0)
     def _():
-        for step in range(1 + SWEEPS):
+        for step in range(1 + ROUNDS):
             rim_in[step, 0] = jnp.zeros((4, rim), F32)
         features[rows : rows + rim] = jnp.zeros((rim, channels), BF16)
         for layer in range(1, layers):
@@ -330,17 +377,35 @@
 
     @pl.when(p == n - 1)
     def _():
-        for step in range(1 + SWEEPS):
+        for step in range(1 + ROUNDS):
             rim_in[step, 1] = jnp.zeros((4, rim), F32)
         features[rows + rim :] = jnp.zeros((rim, channels), BF16)
         for layer in range(1, layers):
             tables[layer, rows + rim :] = jnp.zeros((rim, channels), BF16)
 
+    def clear(side, away):
+        for step in range(1 + ROUNDS):
+            far_in[step, side] = jnp.zeros((4, rim), F32)
+            if away == 1:
+                flat_in[step, side] = jnp.zeros((4, rows), F32)
+        if away == 1:
+            lists_in[side] = jnp.zeros((slots, rim), jnp.int32)
+            fixed_in[side] = jnp.zeros((4, rim), F32)
+
+    @pl.when(g == 1)
+    def _():
+        flat_out[0] = own[0:4]
+        fill(lists_out, neighbours[...])
+        for side, ends in enumerate(((0, 1), (n - 1, n - 2))):
+            pl.when(p == ends[0])(functools.partial(clear, side, 1))
+            pl.when(p == ends[1])(functools.partial(clear, side, 2))
+
     @pl.when(g == 0)
     def _():
         prepare()
 
-    pl.semaphore_wait(barrier, n + (p > 0).astype(jnp.int32) + (p < n - 1).astype(jnp.int32))
+    sides = [p > 0, p < n - 1, p > 1, p < n - 2]
+    pl.semaphore_wait(barrier, n + sum(side.astype(jnp.int32) for side in sides))
 
     def packet_copy(i):
         return pltpu.make_async_remote_copy(
@@ -353,6 +418,12 @@
         )
 
     start(rim_copy, 0)
+
+    @pl.when(g == 1)
+    def _():
+        start(flat_copy, 0)
+        start(far_copy, 0, 2)
+        start(list_copy, 0)
 
     @pl.loop(0, n, unroll=4)
     def _(i):
@@ -412,6 +483,13 @@
         sums = lax.fori_loop(0, rows // 8, step, (zero, zero, zero), unroll=True)
         for c in range(3):
             terms[c : c + 1, :] = jnp.sum(sums[c], axis=0, keepdims=True)
+
+    def lent_pieces(side, c, flat, mine, far):
+        flat, mine, far = (rows_[c : c + 1, :] for rows_ in (flat, mine, far))
+        rims = (far, mine) if side == 0 else (mine, far)
+        return [(b, flat[:, b * BLOCK : (b + 1) * BLOCK]) for b in range(own_blocks)] + [
+            (own_blocks + i, rims[i]) for i in range(2)
+        ]
 
     def edges():
         for tile in range(own_blocks):
@@ -436,7 +514,7 @@
         for q in range(groups):
             parts = []
             for j in range(pack):
-                away = jnp.broadcast_to(geometry[0, q * pack + j : q * pack + j + 1, :], (basis, rows))
+                away = jnp.broadcast_to(geometry[0, q * pack + j : q * pack + j + 1, 0:rows], (basis, rows))
                 away = away - centre
                 parts.append(jnp.exp(-(away * away)))
             turned = jnp.concatenate(parts, axis=0).T
@@ -516,6 +594,32 @@
                 pairs[c : c + 1, at] = extra
             geometry[3, :, at] = w3
             geometry[4, :, at] = 3.0 * (w3 * w2)
+        arrive(flat_copy, 0)
+        arrive(far_copy, 0, 2)
+        arrive(list_copy, 0)
+        for side in range(2):
+            at = slice(rows + side * rim, rows + (side + 1) * rim)
+            index = lists_in[side]
+            local = index & (BLOCK - 1)
+            chunk = lax.shift_right_logical(index, 7)
+            offset = [
+                rim_in[0, side, c : c + 1, :]
+                - table_gather(
+                    lent_pieces(side, c, flat_in[0, side], rim_out[0, 1 - side], far_in[0, side]),
+                    local,
+                    chunk,
+                )
+                for c in range(3)
+            ]
+            w = lax.rsqrt(
+                offset[0] * offset[0] + offset[1] * offset[1] + offset[2] * offset[2] + SMOOTH
+            )
+            w2 = w * w
+            w3 = w2 * w
+            for c in range(3):
+                geometry[c, :, at] = offset[c]
+            geometry[3, :, at] = w3
+            geometry[4, :, at] = 3.0 * (w3 * w2)
 
     pltpu.make_async_copy(everyone, everyone, all_recv).wait()
     for l in range(listed):
@@ -638,55 +742,89 @@
         gain = polar[...]
         outside[...] = outside[...] + pairs[...]
         dipole = [gain * outside[c : c + 1, :] for c in range(3)]
-        for sweep in range(SWEEPS):
+
+        def induced(at, index, pieces, begun=(None, None, None)):
+            local = index & (BLOCK - 1)
+            chunk = lax.shift_right_logical(index, 7)
+            d = [table_gather(pieces(c), local, chunk, begun[c]) for c in range(3)]
+            r = [geometry[c, :, at] for c in range(3)]
+            w3 = geometry[3, :, at]
+            s = (r[0] * d[0] + r[1] * d[1] + r[2] * d[2]) * geometry[4, :, at]
+            return [jnp.sum(r[c] * s - d[c] * w3, axis=0, keepdims=True) for c in range(3)]
+
+        def own_pieces(c, values):
+            return [(b, values[c][:, b * BLOCK : (b + 1) * BLOCK]) for b in range(own_blocks)]
+
+        def own_sweep(values, rims, begun):
+            fresh = [[], [], []]
+            for tile in range(own_blocks):
+                at = slice(tile * BLOCK, (tile + 1) * BLOCK)
+
+                def pieces(c):
+                    ends = [(own_blocks + side, rims(side, c)) for side in range(2)]
+                    return ends if begun else own_pieces(c, values) + ends
+
+                totals = induced(
+                    at, neighbours[:, at], pieces, begun[tile] if begun else (None, None, None)
+                )
+                for c in range(3):
+                    fresh[c].append(gain[:, at] * (outside[c : c + 1, at] + totals[c]))
+            return [jnp.concatenate(f, axis=1) for f in fresh]
+
+        for sweep in range(ROUNDS):
             step = 1 + sweep
-            fill_rims(step, jnp.concatenate(dipole + [jnp.zeros((1, rows), F32)], axis=0))
+            values = jnp.concatenate(dipole + [jnp.zeros((1, rows), F32)], axis=0)
+            fill_rims(step, values)
             start(rim_copy, step)
-            near_part = []
+            start(far_copy, step, 2)
+            flat_out[step] = values
+            start(flat_copy, step)
+            if sweep == 0:
+                fill(fixed_out, jnp.concatenate([outside[...], gain], axis=0))
+                start(fixed_copy, 0)
+            begun = []
             for tile in range(own_blocks):
                 index = neighbours[:, tile * BLOCK : (tile + 1) * BLOCK]
                 local = index & (BLOCK - 1)
                 chunk = lax.shift_right_logical(index, 7)
-                near_part.append([
-                    table_gather(
-                        [(b, dipole[c][:, b * BLOCK : (b + 1) * BLOCK]) for b in range(own_blocks)],
-                        local,
-                        chunk,
-                    )
-                    for c in range(3)
-                ])
+                begun.append([table_gather(own_pieces(c, dipole), local, chunk) for c in range(3)])
             if sweep == 0:
                 term_geometry(True, 0, 1)
             arrive(rim_copy, step)
-            fresh = [[], [], []]
-            for tile in range(own_blocks):
-                at = slice(tile * BLOCK, (tile + 1) * BLOCK)
-                index = neighbours[:, at]
-                local = index & (BLOCK - 1)
-                chunk = lax.shift_right_logical(index, 7)
-                d = [
-                    table_gather(
-                        [(own_blocks + side, rim_in[step, side, c : c + 1, :]) for side in range(2)],
-                        local,
-                        chunk,
-                        near_part[tile][c],
-                    )
+            arrive(far_copy, step, 2)
+            arrive(flat_copy, step)
+            if sweep == 0:
+                arrive(fixed_copy, 0)
+            middle = own_sweep(
+                dipole, lambda side, c: rim_in[step, side, c : c + 1, :], begun
+            )
+            lent_middle = []
+            for side in range(2):
+                at = slice(rows + side * rim, rows + (side + 1) * rim)
+                totals = induced(
+                    at,
+                    lists_in[side],
+                    lambda c: lent_pieces(
+                        side, c, flat_in[step, side], rim_out[step, 1 - side], far_in[step, side]
+                    ),
+                )
+                lent_middle.append([
+                    fixed_in[side, 3:4, :] * (fixed_in[side, c : c + 1, :] + totals[c])
                     for c in range(3)
-                ]
-                r = [geometry[c, :, at] for c in range(3)]
-                w3 = geometry[3, :, at]
-                s = (r[0] * d[0] + r[1] * d[1] + r[2] * d[2]) * geometry[4, :, at]
-                for c in range(3):
-                    total = jnp.sum(r[c] * s - d[c] * w3, axis=0, keepdims=True)
-                    fresh[c].append(gain[:, at] * (outside[c : c + 1, at] + total))
-            dipole = [jnp.concatenate(f, axis=1) for f in fresh]
+                ])
+            dipole = own_sweep(middle, lambda side, c: lent_middle[side][c], None)
         for c in range(3):
             site_result[c : c + 1, :] = dipole[c]
         stacked = jnp.concatenate(dipole + [jnp.zeros((5, rows), F32)], axis=0)
         extra_cols[...] = stacked.T
         send_terms(True)
-        for sweep in range(SWEEPS):
-            gone(rim_copy, 1 + sweep)
+        for step in range(1 + ROUNDS):
+            if step:
+                gone(rim_copy, step)
+            gone(far_copy, step, 2)
+            gone(flat_copy, step)
+        gone(list_copy, 0)
+        gone(fixed_copy, 0)
 
     @pl.loop(0, n, unroll=min(n, 16))
     def _(q):
@@ -784,9 +922,16 @@
             pltpu.VMEM((8, rows), F32),
             pltpu.VMEM((rows, 8), F32),
             pltpu.VMEM((rows, 8), F32),
-            pltpu.VMEM((1 + SWEEPS, 2, 4, rim), F32),
-            pltpu.VMEM((1 + SWEEPS, 2, 4, rim), F32),
-            pltpu.VMEM((5, slots, rows), F32),
+            pltpu.VMEM((1 + ROUNDS, 2, 4, rim), F32),
+            pltpu.VMEM((1 + ROUNDS, 2, 4, rim), F32),
+            pltpu.VMEM((1 + ROUNDS, 4, rows), F32),
+            pltpu.VMEM((1 + ROUNDS, 2, 4, rows), F32),
+            pltpu.VMEM((1 + ROUNDS, 2, 4, rim), F32),
+            pltpu.VMEM((2, slots, rim), jnp.int32),
+            pltpu.VMEM((2, slots, rim), jnp.int32),
+            pltpu.VMEM((2, 4, rim), F32),
+            pltpu.VMEM((2, 4, rim), F32),
+            pltpu.VMEM((5, slots, rows + 2 * rim), F32),
             pltpu.VMEM((pack, rows // STRIP, slots // pack, STRIP, rows + 2 * rim), BF16),
             pltpu.VMEM((2 * rim, rows), BF16),
             pltpu.VMEM((slots // pack * rows, pack * basis), BF16),
@@ -809,12 +954,20 @@
             pltpu.VMEM((n, own_blocks * 3, BLOCK), F32),
             dma(()),
             dma(()),
-            dma((1 + SWEEPS, 2)),
-            dma((1 + SWEEPS, 2)),
+            dma((1 + ROUNDS, 2)),
+            dma((1 + ROUNDS, 2)),
             dma((layers, 2)),
             dma((layers, 2)),
             dma(()),
             dma(()),
+            dma((1 + ROUNDS, 2)),
+            dma((1 + ROUNDS, 2)),
+            dma((1 + ROUNDS, 2)),
+            dma((1 + ROUNDS, 2)),
+            dma((1, 2)),
+            dma((1, 2)),
+            dma((1, 2)),
+            dma((1, 2)),
         ],
         compiler_params=pltpu.CompilerParams(
             collective_id=0, has_side_effects=True, vmem_limit_bytes=40 * 2**20

time: 29.7 us -> 27.8 us (0.936)
  the two profiles are of different devices: /device:TPU:0 before, /device:TPU:1 now
where the time goes in v5:
time: 27.8 us; the launch traced here: 27.6 us
  Pallas kernels  26.3 us (95%)
  between operations  0.64 us (2%)
  local copies, waits for them, and re-layouts  0.6 us (2%)
    pallas_call x1, Pallas kernels, local(): pl.pallas_call(functools.partial(kernel, n_dom, n_sub), out_shape=jax.Sha...  26.3 us
    squeeze x1, local copies, waits for them, and re-layouts, local(): return (both[0], both[1])  0.6 us

profile of v5, /device:TPU:1, one launch (start us, length us, event | category | flops | bytes accessed | tf_op | source)
XLA Modules:
  0.0 27.6 jit_solution(2852263241497220612)
XLA Ops:
  0.6 26.3 %shard_map.149 = f32[2,3,256]{2,1,0:T(4,128)S(1)} custom-call(f32[3,256]{1,0:T(4,128)} %refs_0_.1, f32[1,256]{1,0:T(1,128)} %bitcast.10, f32[1,256]{1,0:T(1,128)} %bitcast.11, bf16[256,256]{1,0:T(8,128)(2,1)} %refs_3_.1, s32[32,256]{1,0:T(8,128)} %bitcast.9, s32[2,128]{1,0:T(2,128)} %refs_5_.1, s32[4]{0:T(128)} %refs_6_.1, bf16[2,8,64]{2,1,0:T(8,128)(2,1)} %refs_7_.1, ...), custom_call_target="tpu_custom_call" | custom-call | tf_op jit(solution)/shard_map/pallas_call | solution.py:910
  27.0 0.6 %slice_bitcast_fusion = (f32[3,256]{1,0:T(4,128)}, f32[3,256]{1,0:T(4,128)}) fusion(f32[2,3,256]{2,1,0:T(4,128)S(1)} %shard_map.149), kind=kLoop, calls=%fused_computation | loop fusion | bytes 12288 | tf_op jit(solution)/shard_map/squeeze | solution.py:976

commit v6 on v5

--- a/solution.py
+++ b/solution.py
@@ -294,18 +294,20 @@
         def _():
             copy(step, 1, p - away).wait_send()
 
-    def prepare():
+    def mark_slots(span):
         width = rows + 2 * rim
         lane = lax.broadcasted_iota(jnp.int32, (rows, width), 1).astype(jnp.int16)
         listing = jnp.concatenate(
             [neighbours[...].astype(F32), jnp.zeros((BLOCK - slots, rows), F32)], axis=0
         ).T.astype(jnp.int32)
         one, none = jnp.ones((rows, width), BF16), jnp.zeros((rows, width), BF16)
-        for k in range(slots):
+        for k in span:
             entry = jnp.broadcast_to(listing[:, k : k + 1], (rows, BLOCK)).astype(jnp.int16)
             entry = jnp.concatenate([entry] * (width // BLOCK), axis=1)
             mark = jnp.where(entry == lane, one, none)
             hot[k % pack, :, k // pack] = mark.reshape(strips, STRIP, width)
+
+    def mark_lent():
         lists = jnp.concatenate(
             [send_rows[...].astype(F32), jnp.zeros((6, rim), F32)], axis=0
         ).T.astype(jnp.int32)
@@ -402,7 +404,7 @@
 
     @pl.when(g == 0)
     def _():
-        prepare()
+        mark_slots(range(slots // 2))
 
     sides = [p > 0, p < n - 1, p > 1, p < n - 2]
     pl.semaphore_wait(barrier, n + sum(side.astype(jnp.int32) for side in sides))
@@ -419,19 +421,15 @@
 
     start(rim_copy, 0)
 
-    @pl.when(g == 1)
-    def _():
-        start(flat_copy, 0)
-        start(far_copy, 0, 2)
-        start(list_copy, 0)
-
     @pl.loop(0, n, unroll=4)
     def _(i):
         packet_copy(i).start()
 
     @pl.when(g == 0)
     def _():
+        mark_lent()
         spread()
+        mark_slots(range(slots // 2, slots))
         lend(0, features[0:rows])
 
     own_cols[...] = own.T
@@ -491,109 +489,7 @@
             (own_blocks + i, rims[i]) for i in range(2)
         ]
 
-    def edges():
-        for tile in range(own_blocks):
-            at = slice(tile * BLOCK, (tile + 1) * BLOCK)
-            index = neighbours[:, at]
-            local = index & (BLOCK - 1)
-            chunk = lax.shift_right_logical(index, 7)
-            picked = []
-            for c in range(4):
-                pieces = [
-                    (b, own_rows[c : c + 1, b * BLOCK : (b + 1) * BLOCK])
-                    for b in range(own_blocks)
-                ] + [(own_blocks + side, rim_in[0, side, c : c + 1, :]) for side in range(2)]
-                picked.append(table_gather(pieces, local, chunk))
-            ox, oy, oz = (own_rows[c : c + 1, at] - picked[c] for c in range(3))
-            dist_sq = ox * ox + oy * oy + oz * oz + SMOOTH
-            yield at, (ox, oy, oz), dist_sq, picked[3], local, chunk
-
-    centre = lax.broadcasted_iota(jnp.int32, (basis, rows), 0).astype(F32) * SPACING
-
-    def waves():
-        for q in range(groups):
-            parts = []
-            for j in range(pack):
-                away = jnp.broadcast_to(geometry[0, q * pack + j : q * pack + j + 1, 0:rows], (basis, rows))
-                away = away - centre
-                parts.append(jnp.exp(-(away * away)))
-            turned = jnp.concatenate(parts, axis=0).T
-            wave[q * rows : (q + 1) * rows, :] = turned.astype(BF16)
-
-    def radial_net(layer):
-        half = groups // 2
-        spans = [range(half), range(half, groups)]
-        for step in range(3):
-            for part, span in enumerate(spans):
-                at = slice(span[0] * rows, (span[-1] + 1) * rows)
-                if step == 0:
-                    source, weight = wave[at, :], wide_in[layer]
-                else:
-                    source, weight = stage[step - 1, at, :], wide_mid[layer, step - 1]
-                h = silu_of_half(jnp.dot(source, weight, preferred_element_type=F32)).astype(BF16)
-                if step < 2:
-                    stage[step, at, :] = h
-                else:
-                    for i, q in enumerate(span):
-                        third[layer, :, q] = h[i * rows : (i + 1) * rows].reshape(
-                            strips, STRIP, channels
-                        )
-
-    def edge_part(layer, j):
-        edge_weight[j] = jnp.dot(
-            third[layer].reshape(groups * rows, channels),
-            wide_out[layer, j],
-            preferred_element_type=F32,
-        ).reshape(strips, groups, STRIP, channels)
-
-    def own_part(layer, beside):
-        for j in range(pack):
-            beside(j)
-            if layer or j >= EARLY:
-                edge_part(layer, j)
-            gather_part(layer, j, 0, rows)
-
-    def rim_part(layer):
-        for j in range(pack):
-            gather_part(layer, j, rows, 2 * rim)
-
-    def gather_part(layer, j, first, count):
-        source = jnp.dot(
-            hot[j, :, :, :, first : first + count].reshape(groups * rows, count),
-            tables[layer, first : first + count],
-            preferred_element_type=F32,
-        )
-        product = edge_weight[j] * source.reshape(strips, groups, STRIP, channels)
-        total = jnp.sum(product, axis=1)
-        if first or j:
-            total = acc[...] + total
-        acc[...] = total
-
-    @pl.when(g == 0)
-    def _():
-        arrive(rim_copy, 0)
-        start(lift_copy, 0)
-        for at, _, dist_sq, _, _, _ in edges():
-            geometry[0, :, at] = jnp.sqrt(dist_sq)
-        waves()
-        radial_net(0)
-        for j in range(EARLY):
-            edge_part(0, j)
-
-    @pl.when(g == 1)
-    def _():
-        arrive(rim_copy, 0)
-        for at, offset, dist_sq, source_charge, _, _ in edges():
-            w = lax.rsqrt(dist_sq)
-            w2 = w * w
-            w3 = w2 * w
-            s = source_charge * w3
-            for c in range(3):
-                geometry[c, :, at] = offset[c]
-                extra = jnp.sum(offset[c] * s, axis=0, keepdims=True)
-                pairs[c : c + 1, at] = extra
-            geometry[3, :, at] = w3
-            geometry[4, :, at] = 3.0 * (w3 * w2)
+    def lent_geometry():
         arrive(flat_copy, 0)
         arrive(far_copy, 0, 2)
         arrive(list_copy, 0)
@@ -621,6 +517,129 @@
             geometry[3, :, at] = w3
             geometry[4, :, at] = 3.0 * (w3 * w2)
 
+    def edge_index(tile):
+        index = neighbours[:, tile * BLOCK : (tile + 1) * BLOCK]
+        return index & (BLOCK - 1), lax.shift_right_logical(index, 7)
+
+    def own_edges(count):
+        return [
+            [
+                table_gather(
+                    [(b, own_rows[c : c + 1, b * BLOCK : (b + 1) * BLOCK]) for b in range(own_blocks)],
+                    *edge_index(tile),
+                )
+                for c in range(count)
+            ]
+            for tile in range(own_blocks)
+        ]
+
+    def edges(begun):
+        for tile in range(own_blocks):
+            at = slice(tile * BLOCK, (tile + 1) * BLOCK)
+            local, chunk = edge_index(tile)
+            picked = [
+                table_gather(
+                    [(own_blocks + side, rim_in[0, side, c : c + 1, :]) for side in range(2)],
+                    local,
+                    chunk,
+                    value,
+                )
+                for c, value in enumerate(begun[tile])
+            ]
+            ox, oy, oz = (own_rows[c : c + 1, at] - picked[c] for c in range(3))
+            dist_sq = ox * ox + oy * oy + oz * oz + SMOOTH
+            yield at, (ox, oy, oz), dist_sq, picked[-1]
+
+    centre = lax.broadcasted_iota(jnp.int32, (basis, rows), 0).astype(F32) * SPACING
+
+    def waves():
+        for q in range(groups):
+            parts = []
+            for j in range(pack):
+                away = jnp.broadcast_to(geometry[0, q * pack + j : q * pack + j + 1, 0:rows], (basis, rows))
+                away = away - centre
+                parts.append(jnp.exp(-(away * away)))
+            turned = jnp.concatenate(parts, axis=0).T
+            wave[q * rows : (q + 1) * rows, :] = turned.astype(BF16)
+
+    def radial_net(layer):
+        half = groups // 2
+        spans = [range(half), range(half, groups)]
+        for step in range(3):
+            for part, span in enumerate(spans):
+                at = slice(span[0] * rows, (span[-1] + 1) * rows)
+                if step == 0:
+                    source, weight = wave[at, :], wide_in[layer]
+                else:
+                    source, weight = stage[step - 1, at, :], wide_mid[layer, step - 1]
+                h = silu_of_half(jnp.dot(source, weight, preferred_element_type=F32)).astype(BF16)
+                if step < 2:
+                    stage[step, at, :] = h
+                else:
+                    for i, q in enumerate(span):
+                        third[layer, :, q] = h[i * rows : (i + 1) * rows].reshape(
+                            strips, STRIP, channels
+                        )
+
+    def edge_part(layer, j):
+        edge_weight[j] = jnp.dot(
+            third[layer].reshape(groups * rows, channels),
+            wide_out[layer, j],
+            preferred_element_type=F32,
+        ).reshape(strips, groups, STRIP, channels)
+
+    def own_part(layer, beside):
+        for j in range(pack):
+            beside(j)
+            if layer or j >= EARLY:
+                edge_part(layer, j)
+            gather_part(layer, j, 0, rows)
+
+    def rim_part(layer):
+        for j in range(pack):
+            gather_part(layer, j, rows, 2 * rim)
+
+    def gather_part(layer, j, first, count):
+        source = jnp.dot(
+            hot[j, :, :, :, first : first + count].reshape(groups * rows, count),
+            tables[layer, first : first + count],
+            preferred_element_type=F32,
+        )
+        product = edge_weight[j] * source.reshape(strips, groups, STRIP, channels)
+        total = jnp.sum(product, axis=1)
+        if first or j:
+            total = acc[...] + total
+        acc[...] = total
+
+    @pl.when(g == 0)
+    def _():
+        begun = own_edges(3)
+        arrive(rim_copy, 0)
+        start(lift_copy, 0)
+        for at, _, dist_sq, _ in edges(begun):
+            geometry[0, :, at] = jnp.sqrt(dist_sq)
+        waves()
+        radial_net(0)
+
+    @pl.when(g == 1)
+    def _():
+        begun = own_edges(4)
+        arrive(rim_copy, 0)
+        start(flat_copy, 0)
+        start(far_copy, 0, 2)
+        start(list_copy, 0)
+        for at, offset, dist_sq, source_charge in edges(begun):
+            w = lax.rsqrt(dist_sq)
+            w2 = w * w
+            w3 = w2 * w
+            s = source_charge * w3
+            for c in range(3):
+                geometry[c, :, at] = offset[c]
+                extra = jnp.sum(offset[c] * s, axis=0, keepdims=True)
+                pairs[c : c + 1, at] = extra
+            geometry[3, :, at] = w3
+            geometry[4, :, at] = 3.0 * (w3 * w2)
+
     pltpu.make_async_copy(everyone, everyone, all_recv).wait()
     for l in range(listed):
         tile = everyone[blocks[l]]
@@ -673,6 +692,8 @@
         def lent_field(side):
             return field(rim_in[0, side], lent_cols.at[side], listed * BLOCK)
 
+        for j in range(EARLY):
+            edge_part(0, j)
         strength = strength_of(field(own, near_cols, listed * BLOCK))
         site_result[2:3, :] = strength
         hidden_ref[...] = embed(column_of(strength), slice(0, rows))
@@ -789,6 +810,7 @@
                 chunk = lax.shift_right_logical(index, 7)
                 begun.append([table_gather(own_pieces(c, dipole), local, chunk) for c in range(3)])
             if sweep == 0:
+                lent_geometry()
                 term_geometry(True, 0, 1)
             arrive(rim_copy, step)
             arrive(far_copy, step, 2)

time: 27.8 us -> 27.4 us (0.986)
  Pallas kernels: 26.3 us -> 25.9 us
    pallas_call x1, Pallas kernels: 26.3 us -> 25.9 us  [local(): pl.pallas_call(functools.partial(kernel, n_dom, n_sub), out_shape=jax.Sha...]
where the time goes in v6:
time: 27.4 us; the launch traced here: 27.2 us
  Pallas kernels  25.9 us (95%)
  between operations  0.64 us (2%)
  local copies, waits for them, and re-layouts  0.6 us (2%)
    pallas_call x1, Pallas kernels, local(): pl.pallas_call(functools.partial(kernel, n_dom, n_sub), out_shape=jax.Sha...  25.9 us
    squeeze x1, local copies, waits for them, and re-layouts, local(): return (both[0], both[1])  0.6 us

profile of v6, /device:TPU:1, one launch (start us, length us, event | category | flops | bytes accessed | tf_op | source)
XLA Modules:
  0.0 27.2 jit_solution(4613403097883065217)
XLA Ops:
  0.6 25.9 %shard_map.149 = f32[2,3,256]{2,1,0:T(4,128)S(1)} custom-call(f32[3,256]{1,0:T(4,128)} %refs_0_.1, f32[1,256]{1,0:T(1,128)} %bitcast.10, f32[1,256]{1,0:T(1,128)} %bitcast.11, bf16[256,256]{1,0:T(8,128)(2,1)} %refs_3_.1, s32[32,256]{1,0:T(8,128)} %bitcast.9, s32[2,128]{1,0:T(2,128)} %refs_5_.1, s32[4]{0:T(128)} %refs_6_.1, bf16[2,8,64]{2,1,0:T(8,128)(2,1)} %refs_7_.1, ...), custom_call_target="tpu_custom_call" | custom-call | tf_op jit(solution)/shard_map/pallas_call | solution.py:932
  26.6 0.6 %slice_bitcast_fusion = (f32[3,256]{1,0:T(4,128)}, f32[3,256]{1,0:T(4,128)}) fusion(f32[2,3,256]{2,1,0:T(4,128)S(1)} %shard_map.149), kind=kLoop, calls=%fused_computation | loop fusion | bytes 12288 | tf_op jit(solution)/shard_map/squeeze | solution.py:998

commit v7 on v6

--- a/solution.py
+++ b/solution.py
@@ -224,7 +224,7 @@
         return pltpu.make_async_remote_copy(
             src_ref=src,
             dst_ref=dst,
-            send_sem=send.at[step, side],
+            send_sem=send.at[side],
             recv_sem=recv.at[step, side],
             device_id=place(g, q),
             device_id_type=MESH,
@@ -723,6 +723,7 @@
                 hidden_ref[...], node_in[layer], preferred_element_type=F32
             ).astype(BF16)
             lend(layer, lifted)
+            gone(lift_copy, layer - 1)
             start(lift_copy, layer)
             tables[layer, 0:rows] = lifted
 
@@ -752,8 +753,7 @@
             readout[...], hidden_ref[...], across, preferred_element_type=F32
         )
         send_terms(False)
-        for layer in range(layers):
-            gone(lift_copy, layer)
+        gone(lift_copy, layers - 1)
 
     @pl.when(g == 1)
     def _():
@@ -796,6 +796,9 @@
             step = 1 + sweep
             values = jnp.concatenate(dipole + [jnp.zeros((1, rows), F32)], axis=0)
             fill_rims(step, values)
+            gone(rim_copy, step - 1)
+            gone(far_copy, step - 1, 2)
+            gone(flat_copy, step - 1)
             start(rim_copy, step)
             start(far_copy, step, 2)
             flat_out[step] = values
@@ -840,23 +843,10 @@
         stacked = jnp.concatenate(dipole + [jnp.zeros((5, rows), F32)], axis=0)
         extra_cols[...] = stacked.T
         send_terms(True)
-        for step in range(1 + ROUNDS):
-            if step:
-                gone(rim_copy, step)
-            gone(far_copy, step, 2)
-            gone(flat_copy, step)
+        gone(far_copy, ROUNDS, 2)
+        gone(flat_copy, ROUNDS)
         gone(list_copy, 0)
         gone(fixed_copy, 0)
-
-    @pl.loop(0, n, unroll=min(n, 16))
-    def _(q):
-        for b in range(own_blocks):
-            total = jnp.zeros((3, BLOCK), F32)
-            for l in range(listed):
-                total = total + jnp.where(
-                    blocks[l] == q * own_blocks + b, terms[:, l * BLOCK : (l + 1) * BLOCK], 0.0
-                )
-            term_out[q, b * 3 : (b + 1) * 3, :] = total
 
     def term_copy(i):
         return pltpu.make_async_remote_copy(
@@ -868,9 +858,22 @@
             device_id_type=MESH,
         )
 
-    @pl.loop(0, n, unroll=4)
-    def _(i):
-        term_copy(i).start()
+    for first, last in ((0, n // 2), (n // 2, n)):
+
+        @pl.loop(first, last, unroll=min(n // 2, 8))
+        def _(i):
+            q = peer(i)
+            for b in range(own_blocks):
+                total = jnp.zeros((3, BLOCK), F32)
+                for l in range(listed):
+                    total = total + jnp.where(
+                        blocks[l] == q * own_blocks + b, terms[:, l * BLOCK : (l + 1) * BLOCK], 0.0
+                    )
+                term_out[q, b * 3 : (b + 1) * 3, :] = total
+
+        @pl.loop(first, last, unroll=4)
+        def _(i):
+            term_copy(i).start()
 
     gone(rim_copy, 0)
     pltpu.make_async_copy(everyone, everyone, all_send).wait()
@@ -976,19 +979,19 @@
             pltpu.VMEM((n, own_blocks * 3, BLOCK), F32),
             dma(()),
             dma(()),
+            dma((2,)),
             dma((1 + ROUNDS, 2)),
-            dma((1 + ROUNDS, 2)),
-            dma((layers, 2)),
+            dma((2,)),
             dma((layers, 2)),
             dma(()),
             dma(()),
+            dma((2,)),
             dma((1 + ROUNDS, 2)),
+            dma((2,)),
             dma((1 + ROUNDS, 2)),
-            dma((1 + ROUNDS, 2)),
-            dma((1 + ROUNDS, 2)),
+            dma((2,)),
             dma((1, 2)),
-            dma((1, 2)),
-            dma((1, 2)),
+            dma((2,)),
             dma((1, 2)),
         ],
         compiler_params=pltpu.CompilerParams(

time: 27.4 us -> 27.2 us (level)
  no operation moved by 1% of the time
where the time goes in v7:
time: 27.2 us; the launch traced here: 27 us
  Pallas kernels  25.8 us (95%)
  between operations  0.64 us (2%)
  local copies, waits for them, and re-layouts  0.6 us (2%)
    pallas_call x1, Pallas kernels, local(): pl.pallas_call(functools.partial(kernel, n_dom, n_sub), out_shape=jax.Sha...  25.8 us
    squeeze x1, local copies, waits for them, and re-layouts, local(): return (both[0], both[1])  0.6 us

profile of v7, /device:TPU:1, one launch (start us, length us, event | category | flops | bytes accessed | tf_op | source)
XLA Modules:
  0.0 27.0 jit_solution(4270407155201513425)
XLA Ops:
  0.6 25.8 %shard_map.149 = f32[2,3,256]{2,1,0:T(4,128)S(1)} custom-call(f32[3,256]{1,0:T(4,128)} %refs_0_.1, f32[1,256]{1,0:T(1,128)} %bitcast.10, f32[1,256]{1,0:T(1,128)} %bitcast.11, bf16[256,256]{1,0:T(8,128)(2,1)} %refs_3_.1, s32[32,256]{1,0:T(8,128)} %bitcast.9, s32[2,128]{1,0:T(2,128)} %refs_5_.1, s32[4]{0:T(128)} %refs_6_.1, bf16[2,8,64]{2,1,0:T(8,128)(2,1)} %refs_7_.1, ...), custom_call_target="tpu_custom_call" | custom-call | tf_op jit(solution)/shard_map/pallas_call | solution.py:935
  26.4 0.6 %slice_bitcast_fusion = (f32[3,256]{1,0:T(4,128)}, f32[3,256]{1,0:T(4,128)}) fusion(f32[2,3,256]{2,1,0:T(4,128)S(1)} %shard_map.149), kind=kLoop, calls=%fused_computation | loop fusion | bytes 12288 | tf_op jit(solution)/shard_map/squeeze | solution.py:1001

commit v8 on v7

--- a/solution.py
+++ b/solution.py
@@ -15,7 +15,7 @@
 MESH = pl.DeviceIdType.MESH
 INPUTS = 14
 STRIP = 16
-EARLY = 2
+EARLY = 3
 F32 = jnp.float32
 BF16 = jnp.bfloat16
 
@@ -614,8 +614,8 @@
     @pl.when(g == 0)
     def _():
         begun = own_edges(3)
+        start(lift_copy, 0)
         arrive(rim_copy, 0)
-        start(lift_copy, 0)
         for at, _, dist_sq, _ in edges(begun):
             geometry[0, :, at] = jnp.sqrt(dist_sq)
         waves()

time: 27.2 us -> 27.1 us (level)
  no operation moved by 1% of the time
where the time goes in v8:
time: 27.1 us; the launch traced here: 26.9 us
  Pallas kernels  25.7 us (95%)
  between operations  0.64 us (2%)
  local copies, waits for them, and re-layouts  0.6 us (2%)
    pallas_call x1, Pallas kernels, local(): pl.pallas_call(functools.partial(kernel, n_dom, n_sub), out_shape=jax.Sha...  25.7 us
    squeeze x1, local copies, waits for them, and re-layouts, local(): return (both[0], both[1])  0.6 us

profile of v8, /device:TPU:1, one launch (start us, length us, event | category | flops | bytes accessed | tf_op | source)
XLA Modules:
  0.0 26.9 jit_solution(164877452359595856)
XLA Ops:
  0.6 25.7 %shard_map.149 = f32[2,3,256]{2,1,0:T(4,128)S(1)} custom-call(f32[3,256]{1,0:T(4,128)} %refs_0_.1, f32[1,256]{1,0:T(1,128)} %bitcast.10, f32[1,256]{1,0:T(1,128)} %bitcast.11, bf16[256,256]{1,0:T(8,128)(2,1)} %refs_3_.1, s32[32,256]{1,0:T(8,128)} %bitcast.9, s32[2,128]{1,0:T(2,128)} %refs_5_.1, s32[4]{0:T(128)} %refs_6_.1, bf16[2,8,64]{2,1,0:T(8,128)(2,1)} %refs_7_.1, ...), custom_call_target="tpu_custom_call" | custom-call | tf_op jit(solution)/shard_map/pallas_call | solution.py:935
  26.3 0.6 %slice_bitcast_fusion = (f32[3,256]{1,0:T(4,128)}, f32[3,256]{1,0:T(4,128)}) fusion(f32[2,3,256]{2,1,0:T(4,128)S(1)} %shard_map.149), kind=kLoop, calls=%fused_computation | loop fusion | bytes 12288 | tf_op jit(solution)/shard_map/squeeze | solution.py:1001

commit v9 on v8

--- a/solution.py
+++ b/solution.py
@@ -563,8 +563,8 @@
             wave[q * rows : (q + 1) * rows, :] = turned.astype(BF16)
 
     def radial_net(layer):
-        half = groups // 2
-        spans = [range(half), range(half, groups)]
+        quarter = max(groups // 4, 1)
+        spans = [range(q, q + quarter) for q in range(0, groups, quarter)]
         for step in range(3):
             for part, span in enumerate(spans):
                 at = slice(span[0] * rows, (span[-1] + 1) * rows)

time: 27.1 us -> 27.1 us (level)
  no operation moved by 1% of the time
where the time goes in v9:
time: 27.1 us; the launch traced here: 26.9 us
  Pallas kernels  25.7 us (95%)
  between operations  0.64 us (2%)
  local copies, waits for them, and re-layouts  0.6 us (2%)
    pallas_call x1, Pallas kernels, local(): pl.pallas_call(functools.partial(kernel, n_dom, n_sub), out_shape=jax.Sha...  25.7 us
    squeeze x1, local copies, waits for them, and re-layouts, local(): return (both[0], both[1])  0.6 us

profile of v9, /device:TPU:1, one launch (start us, length us, event | category | flops | bytes accessed | tf_op | source)
XLA Modules:
  0.0 26.9 jit_solution(14397144475648750511)
XLA Ops:
  0.6 25.7 %shard_map.149 = f32[2,3,256]{2,1,0:T(4,128)S(1)} custom-call(f32[3,256]{1,0:T(4,128)} %refs_0_.1, f32[1,256]{1,0:T(1,128)} %bitcast.10, f32[1,256]{1,0:T(1,128)} %bitcast.11, bf16[256,256]{1,0:T(8,128)(2,1)} %refs_3_.1, s32[32,256]{1,0:T(8,128)} %bitcast.9, s32[2,128]{1,0:T(2,128)} %refs_5_.1, s32[4]{0:T(128)} %refs_6_.1, bf16[2,8,64]{2,1,0:T(8,128)(2,1)} %refs_7_.1, ...), custom_call_target="tpu_custom_call" | custom-call | tf_op jit(solution)/shard_map/pallas_call | solution.py:935
  26.3 0.6 %slice_bitcast_fusion = (f32[3,256]{1,0:T(4,128)}, f32[3,256]{1,0:T(4,128)}) fusion(f32[2,3,256]{2,1,0:T(4,128)S(1)} %shard_map.149), kind=kLoop, calls=%fused_computation | loop fusion | bytes 12288 | tf_op jit(solution)/shard_map/squeeze | solution.py:1001
